TPU v7x, 32 devices: a whole 2x2x4 slice. The times are simulated.
32 devices in a mesh: graph: 8 (over z, y), mp: 4 (over x, core).
Axes of the slice: x: 2, y: 2, z: 4, core: 2. Of those that a mesh axis runs over, the one named last changes fastest.
Arguments:
- node_features: bfloat16 [16, 128, 1024], P('graph'), may hold values from -24 to 24
- wq: bfloat16 [1024, 4, 256], P(None, 'mp'), may hold values from -0.375 to 0.375
- wkv: bfloat16 [1024, 4, 128], P(None, 'mp'), may hold values from -0.1875 to 0.1875
- wo: bfloat16 [4, 256, 1024], P('mp'), may hold values from -0.1875 to 0.1875
- send_list: int32 [8, 8, 1], P('graph'), may hold values from 0 to 1
- block_list: int32 [16, 32], P('graph'), may hold values from 0 to 7, as said below
- cotangent: bfloat16 [2048, 1024], P('graph'), may hold values from -0.75 to 0.75
Outputs:
- layer_output: bfloat16 [2048, 1024], P(('graph', 'mp'))
- grad_wq: float32 [1024, 4, 256], P('graph', 'mp')
- grad_wkv: float32 [1024, 4, 128], P('graph', 'mp')
- grad_wo: float32 [4, 256, 1024], P('mp', None, 'graph')
Inputs may be any that keep to these rules, and one draw needn't show every extreme that they name: `send_list`: each entry is a tile index local to the sending partition. `block_list`: entry b names slot b % 1 filled by partition b // 1 for the query tile's partition. The entries of one partition's tiles, read row by row, run through a random order of all 8 slot numbers and then start that order again.
All inputs are finite; a program needn't handle non-finite values.
Results may differ from a plain program's by a relative error of at most 0.0035.
The roundings to bfloat16 on the way count: a program that leaves them out, or rounds other values in their place, can miss the bound.
Values may be sent and summed in bfloat16 or wider, within the bound.
No kernel may reach another device: no remote copies, remote signals or barrier semaphores. Data moves between devices by JAX's collectives and lax.ppermute only.
A program may use at most 64 MiB of HBM per device.

v0:
```python
import jax
import jax.numpy as jnp
from jax import lax
from jax.experimental import pallas as pl
from jax.experimental.pallas import tpu as pltpu
from jax.sharding import PartitionSpec as P

DH = 64
F32 = jnp.float32
BF16 = jnp.bfloat16


def head_forward(query_head, key_flat, width):
    score = jnp.einsum(
        "rhd,khd->hrk", query_head, key_flat[..., :width], preferred_element_type=F32
    )
    row_max = jnp.max(score, axis=-1, keepdims=True)
    exponent = jnp.exp(score - row_max)
    weights = exponent / jnp.sum(exponent, axis=-1, keepdims=True)
    rounded = weights.astype(BF16)
    mixed = jnp.einsum(
        "hrk,khd->rhd", rounded, key_flat[..., width:], preferred_element_type=F32
    ).astype(BF16)
    return (weights, rounded, mixed)


def tile_forward(query_tile, key_rows):
    heads = query_tile.shape[1]
    width = query_tile.shape[3]
    key_flat = key_rows.reshape(-1, heads, 2 * width)

    def one_head(query_head):
        return head_forward(query_head, key_flat, width)[2]

    per_head = lax.map(one_head, jnp.moveaxis(query_tile, 2, 0))
    return jnp.moveaxis(per_head, 0, 2)


def tile_backward(query_tile, key_rows, grad_tile):
    heads = query_tile.shape[1]
    width = query_tile.shape[3]
    key_flat = key_rows.reshape(-1, heads, 2 * width)

    def one_head(total, entry):
        query_head, grad_head = entry
        weights, rounded, _ = head_forward(query_head, key_flat, width)
        grad_prob = jnp.einsum(
            "rhd,khd->hrk", grad_head, key_flat[..., width:], preferred_element_type=F32
        )
        delta = jnp.sum(weights * grad_prob, axis=-1, keepdims=True)
        grad_score = (weights * (grad_prob - delta)).astype(BF16)
        grad_query = (
            jnp.einsum(
                "hrk,khd->rhd", grad_score, key_flat[..., :width], preferred_element_type=F32
            )
            * width ** (-0.5)
        ).astype(BF16)
        grad_key = jnp.einsum("hrk,rhd->khd", grad_score, query_head, preferred_element_type=F32)
        grad_value = jnp.einsum("hrk,rhd->khd", rounded, grad_head, preferred_element_type=F32)
        total = total + jnp.concatenate([grad_key, grad_value], axis=-1)
        return (total, grad_query)

    start_total = jnp.zeros(key_flat.shape, F32)
    key_grad, grad_query = lax.scan(
        one_head, start_total, (jnp.moveaxis(query_tile, 2, 0), jnp.moveaxis(grad_tile, 2, 0))
    )
    return (jnp.moveaxis(grad_query, 0, 2), key_grad.reshape(key_rows.shape))


def listed_local(node_features, wq, wkv, wo, send_list, block_list, cotangent):
    tiles, tile_rows, width = node_features.shape
    heads = wq.shape[1]
    head_width = wq.shape[2]
    groups = head_width // DH
    parts = lax.axis_size("graph")
    slots = send_list.shape[2]
    token_rows = node_features.reshape(tiles * tile_rows, width)
    query = (
        jnp.dot(token_rows, wq.reshape(width, -1), preferred_element_type=F32) * DH ** (-0.5)
    ).astype(BF16)
    query = query.reshape(tiles, tile_rows, heads, groups, DH)
    keyval = jnp.dot(token_rows, wkv.reshape(width, -1), preferred_element_type=F32).astype(BF16)
    keyval = keyval.reshape(tiles, tile_rows, -1)
    outgoing = keyval[send_list[0].reshape(-1)]
    received = lax.all_to_all(outgoing, "graph", split_axis=0, concat_axis=0, tiled=True)

    def forward_one(entry):
        query_tile, key_ids = entry
        return tile_forward(query_tile, received[key_ids])

    mixed = lax.map(forward_one, (query, block_list))
    mixed_rows = mixed.reshape(tiles * tile_rows, heads * head_width)
    out_flat = wo.reshape(heads * head_width, width)
    share = tiles * tile_rows // lax.axis_size("mp")
    summed = lax.psum_scatter(
        jnp.dot(mixed_rows, out_flat, preferred_element_type=F32),
        "mp",
        scatter_dimension=0,
        tiled=True,
    )
    own_rows = lax.dynamic_slice_in_dim(token_rows, lax.axis_index("mp") * share, share, 0)
    output = (own_rows.astype(F32) + summed).astype(BF16)
    grad_out_local = jnp.dot(mixed_rows.T, cotangent, preferred_element_type=F32).reshape(wo.shape)
    grad_mixed = jnp.einsum("rd,hd->rh", cotangent, out_flat, preferred_element_type=F32).astype(
        BF16
    )
    grad_mixed = grad_mixed.reshape(tiles, tile_rows, heads, groups, DH)

    def backward_one(entry):
        query_tile, key_ids, grad_tile = entry
        return tile_backward(query_tile, received[key_ids], grad_tile)

    grad_query, key_grad = lax.map(backward_one, (query, block_list, grad_mixed))
    slot_ids = jnp.arange(parts * slots, dtype=jnp.int32)
    picks = (block_list.reshape(1, -1) == slot_ids[:, None]).astype(F32)
    slot_grad = jnp.dot(
        picks,
        key_grad.reshape(tiles * block_list.shape[1], -1),
        precision=lax.Precision.HIGHEST,
        preferred_element_type=F32,
    ).astype(BF16)
    slot_grad = slot_grad.reshape(parts * slots, tile_rows, -1)
    returned = lax.all_to_all(slot_grad, "graph", split_axis=0, concat_axis=0, tiled=True)
    owners = (send_list[0].reshape(1, -1) == jnp.arange(tiles, dtype=jnp.int32)[:, None]).astype(
        BF16
    )
    grad_keyval = jnp.dot(
        owners, returned.reshape(parts * slots, -1), preferred_element_type=F32
    ).astype(BF16)
    grad_keyval = grad_keyval.reshape(tiles * tile_rows, -1)
    grad_query_local = jnp.dot(
        token_rows.T, grad_query.reshape(tiles * tile_rows, -1), preferred_element_type=F32
    ).reshape(wq.shape)
    grad_keyval_local = jnp.dot(token_rows.T, grad_keyval, preferred_element_type=F32).reshape(
        wkv.shape
    )
    grad_wq = lax.psum_scatter(grad_query_local, "graph", scatter_dimension=0, tiled=True)
    grad_wkv = lax.psum_scatter(grad_keyval_local, "graph", scatter_dimension=0, tiled=True)
    grad_out = lax.psum_scatter(grad_out_local, "graph", scatter_dimension=2, tiled=True)
    return (output, grad_wq, grad_wkv, grad_out)


def dot(a, b, contract=((1,), (0,))):
    return lax.dot_general(a, b, (contract, ((), ())), preferred_element_type=F32)


NT = ((1,), (1,))


def keyval_kernel(send_ref, x_ref, wkv_ref, out_ref, kv_ref):
    rows = out_ref.shape[1]
    kv = dot(x_ref[...], wkv_ref[...]).astype(BF16)
    for t in range(kv_ref.shape[0]):
        kv_ref[t] = kv[t * rows : (t + 1) * rows]
    for r in range(out_ref.shape[0]):
        out_ref[r] = kv_ref[send_ref[r]]


def project_kernel(x_ref, wq_ref, wo_ref, cot_ref, w_ref, half_ref):
    tokens = x_ref.shape[0]
    groups = w_ref.shape[0]
    query = (dot(x_ref[...], wq_ref[...]) * DH ** (-0.5)).astype(BF16)
    query_t = query.T
    grad_mixed_t = dot(wo_ref[...], cot_ref[...], NT).astype(BF16)
    w_ref[...] = jnp.zeros_like(w_ref)
    for k in range(groups):
        w_ref[k, :DH, :tokens] = query_t[k * DH : (k + 1) * DH]
        w_ref[k, DH:, tokens:] = grad_mixed_t[k * DH : (k + 1) * DH]
    other = 1 - lax.rem(lax.axis_index("graph"), 2)
    outer = half_ref.shape[1]
    cols = half_ref.shape[3]
    for d in range(outer):
        at = pl.ds(pl.multiple_of((2 * d + other) * cols, cols), cols)
        half_ref[0, d] = cot_ref[:, at]
        half_ref[1, d] = x_ref[:, at]


def attention_kernel(w_ref, kv_ref, slot_ref, mix_ref, acc_ref):
    groups, _, twice = w_ref.shape
    tokens = twice // 2
    scale = DH ** (-0.5)
    kv = kv_ref[...]
    kv_t = kv.T
    acc_ref[...] = jnp.zeros_like(acc_ref)

    def group(k, carry):
        weights = w_ref[k]
        both = dot(kv, weights)
        score, grad_prob = both[:, :tokens], both[:, tokens:]
        exponent = jnp.exp(score - jnp.max(score, axis=0, keepdims=True))
        prob = exponent * (1.0 / jnp.sum(exponent, axis=0, keepdims=True))
        delta = jnp.sum(prob * grad_prob, axis=0, keepdims=True)
        rounded = prob.astype(BF16)
        grad_score = (prob * (grad_prob - delta)).astype(BF16)
        pair = jnp.concatenate([grad_score, rounded], axis=1)
        outs = dot(kv_t, pair)
        mix_ref[0, k] = outs[DH:, tokens:].astype(BF16)
        mix_ref[1, k] = (outs[:DH, :tokens] * scale).astype(BF16)
        acc_ref[...] += dot(pair, weights, NT)
        return carry

    lax.fori_loop(0, groups, group, 0)
    slot_ref[...] = acc_ref[...].astype(BF16)


def output_kernel(mix_ref, wo_ref, out_keep_ref, out_send_ref):
    mp = lax.axis_index("mp")
    core, across = lax.rem(mp, 2), lax.div(mp, 2)
    rows = out_keep_ref.shape[1]
    mixed = mix_ref[0].T
    part = dot(mixed, wo_ref[...])
    for m in range(4):
        block = part[m * rows : (m + 1) * rows]
        place = lax.bitwise_xor(m // 2, across)

        @pl.when(core == m % 2)
        def _():
            out_keep_ref[place] = block

        @pl.when(core != m % 2)
        def _():
            out_send_ref[place] = block


def exponent_of(peak):
    return jnp.ceil(jnp.log2(jnp.maximum(peak, 1e-30))) - 14.0


def peak_of(value, peak):
    top = jnp.max(jnp.abs(value), axis=0, keepdims=True)
    return jnp.maximum(peak, jnp.max(top, axis=1, keepdims=True))


def weights_kernel(mix_ref, mix_got_ref, cot_ref, x_ref, half_ref, own_ref, *out_refs):
    graph = lax.axis_index("graph")
    y, z = lax.rem(graph, 2), lax.div(graph, 2)
    head_width = mix_ref.shape[1]
    cols = half_ref.shape[3]
    parts = head_width // cols
    refs = (own_ref,) + out_refs
    peak = jnp.zeros((1, 1), F32)
    for d, ref in enumerate(refs):
        there = lax.bitwise_xor(z, d)
        at = pl.ds(pl.multiple_of((2 * there + y) * cols, cols), cols)
        wo = dot(mix_ref[0], cot_ref[:, at]) + dot(mix_got_ref[0], half_ref[0, there])
        wq = dot(mix_ref[1], x_ref[:, at]) + dot(mix_got_ref[1], half_ref[1, there])
        ref[:head_width] = wo
        for h in range(parts):
            place = pl.ds(head_width + h, cols, parts)
            ref[place, :] = wq[h * cols : (h + 1) * cols].T
        if d > 0:
            peak = peak_of(wo, peak_of(wq, peak))
    e = exponent_of(peak)
    factor = jnp.exp2(-e)
    rows = 2 * head_width
    for ref in out_refs:
        ref[:rows] = ref[:rows] * factor
        ref[rows:] = jnp.broadcast_to(e, ref[rows:].shape)


def owner_kernel(send_ref, ret_ref, x_ref, out_ref):
    receivers, rows = ret_ref.shape[:2]
    tiles = x_ref.shape[0] // rows
    sums = []
    for t in range(tiles):
        total = jnp.zeros(ret_ref.shape[1:], F32)
        for r in range(receivers):
            mine = (send_ref[r] == t).astype(F32)
            total += ret_ref[r].astype(F32) * mine
        sums.append(total.astype(BF16))
    grad_kv_t = jnp.concatenate(sums, axis=0).T
    cols = out_ref.shape[2]
    kv_width = grad_kv_t.shape[0]
    whole = dot(grad_kv_t, x_ref[...])
    e = exponent_of(peak_of(whole, jnp.zeros((1, 1), F32)))
    factor = jnp.exp2(-e)
    for r in range(out_ref.shape[0]):
        out_ref[r, :kv_width] = whole[:, r * cols : (r + 1) * cols].T * factor
        out_ref[r, kv_width:] = jnp.broadcast_to(e, out_ref[r, kv_width:].shape)


def unscaled(got):
    rows = got.shape[-2] - 16
    return got[..., :rows, :].astype(F32) * jnp.exp2(got[..., rows : rows + 1, :1].astype(F32))


def vmem(count):
    return [pl.BlockSpec(memory_space=pltpu.VMEM)] * count


SMEM = pl.BlockSpec(memory_space=pltpu.SMEM)


def xor_pairs(n, k):
    return [(i, i ^ k) for i in range(n)]


def shared_local(node_features, wq, wkv, wo, send_list, block_list, cotangent):
    tiles, rows, width = node_features.shape
    tokens = tiles * rows
    head_width = wq.shape[1] * wq.shape[2]
    kv_width = wkv.shape[2]
    groups = head_width // DH
    parts = lax.axis_size("graph")
    mp = lax.axis_size("mp")
    cols = width // parts
    x = node_features.reshape(tokens, width)
    send = send_list.reshape(-1)
    wq2, wkv2 = wq.reshape(width, head_width), wkv.reshape(width, kv_width)
    wo2 = wo.reshape(head_width, width)

    outgoing = pl.pallas_call(
        keyval_kernel,
        out_shape=jax.ShapeDtypeStruct((parts, rows, kv_width), BF16),
        in_specs=[SMEM] + vmem(2),
        out_specs=vmem(1)[0],
        scratch_shapes=[pltpu.VMEM((tiles, rows, kv_width), BF16)],
        name="keyval",
    )(send, x, wkv2)
    received = lax.all_to_all(outgoing, "graph", split_axis=0, concat_axis=0, tiled=True)
    keys = parts * rows
    share = tokens // mp
    outer = parts // 2
    weights, half = pl.pallas_call(
        project_kernel,
        out_shape=(
            jax.ShapeDtypeStruct((groups, kv_width, 2 * tokens), BF16),
            jax.ShapeDtypeStruct((2, outer, tokens, cols), BF16),
        ),
        in_specs=vmem(4),
        out_specs=tuple(vmem(2)),
        name="project",
    )(x, wq2, wo2, cotangent)
    half_got = lax.ppermute(half, "graph", xor_pairs(parts, 1))
    slot_grad, mix = pl.pallas_call(
        attention_kernel,
        out_shape=(
            jax.ShapeDtypeStruct((keys, kv_width), BF16),
            jax.ShapeDtypeStruct((2, groups, DH, tokens), BF16),
        ),
        in_specs=vmem(2),
        out_specs=tuple(vmem(2)),
        scratch_shapes=[pltpu.VMEM((keys, kv_width), F32)],
        name="attention",
    )(weights, received.reshape(keys, kv_width))
    returned = lax.all_to_all(
        slot_grad.reshape(parts, rows, kv_width), "graph", split_axis=0, concat_axis=0, tiled=True
    )
    mix = mix.reshape(2, head_width, tokens)
    mix_got = lax.ppermute(mix, "graph", xor_pairs(parts, 1))
    out_keep, out_away = pl.pallas_call(
        output_kernel,
        out_shape=(
            jax.ShapeDtypeStruct((mp // 2, share, width), F32),
            jax.ShapeDtypeStruct((mp // 2, share, width), F32),
        ),
        in_specs=vmem(2),
        out_specs=tuple(vmem(2)),
        name="output",
    )(mix, wo2)
    out_got = lax.ppermute(out_away, "mp", xor_pairs(mp, 1))
    sums, *sums_away = pl.pallas_call(
        weights_kernel,
        out_shape=tuple(
            jax.ShapeDtypeStruct((2 * head_width + 16 * (d > 0), cols), F32)
            for d in range(outer)
        ),
        in_specs=vmem(5),
        out_specs=tuple(vmem(outer)),
        name="weights",
    )(mix, mix_got, cotangent, x, half_got)
    sums_got = []
    for d in range(1, outer):
        away = sums_away[d - 1].astype(jnp.float16)
        sums_got.append(lax.ppermute(away, "graph", xor_pairs(parts, 2 * d)))
    kv_parts = pl.pallas_call(
        owner_kernel,
        out_shape=jax.ShapeDtypeStruct((parts, kv_width + 16, cols), F32),
        in_specs=[SMEM] + vmem(2),
        out_specs=vmem(1)[0],
        name="owner",
    )(send, returned, x)
    kv_parts = kv_parts.astype(jnp.float16)
    kv_got = lax.all_to_all(kv_parts, "graph", split_axis=0, concat_axis=0, tiled=True)
    out_half = out_keep + out_got
    out_last = lax.ppermute(out_half[1], "mp", xor_pairs(mp, 2))
    own_rows = lax.dynamic_slice_in_dim(x, lax.axis_index("mp") * share, share, 0)
    output = (own_rows.astype(F32) + (out_half[0] + out_last)).astype(BF16)
    for got in sums_got:
        sums = sums + unscaled(got)
    grad_wo, grad_wq = sums[:head_width], sums[head_width:]
    grad_wkv = jnp.sum(unscaled(kv_got), axis=0)
    return (
        output,
        grad_wq.reshape(cols, *wq.shape[1:]),
        grad_wkv.reshape(cols, *wkv.shape[1:]),
        grad_wo.reshape(*wo.shape[:2], cols),
    )


def local(node_features, wq, wkv, wo, send_list, block_list, cotangent):
    parts, mp, slots = lax.axis_size("graph"), lax.axis_size("mp"), send_list.shape[2]
    copies, rest = divmod(block_list.shape[1], parts * slots)
    every_slot = rest == 0 and copies & (copies - 1) == 0
    if every_slot and slots == 1 and parts == 8 and mp == 4 and wq.shape[1] == 1:
        body = shared_local
    else:
        body = listed_local
    return body(node_features, wq, wkv, wo, send_list, block_list, cotangent)


def solution(mesh):
    return jax.shard_map(
        local,
        mesh=mesh,
        in_specs=(
            P("graph", None, None),
            P(None, "mp", None),
            P(None, "mp", None),
            P("mp", None, None),
            P("graph", None, None),
            P("graph", None),
            P("graph", None),
        ),
        out_specs=(
            P(("graph", "mp"), None),
            P("graph", "mp", None),
            P("graph", "mp", None),
            P("mp", None, "graph"),
        ),
        check_vma=False,
    )
```

profile of v0, /device:TPU:0, one launch (start us, length us, event | category | flops | bytes accessed | tf_op | source)
XLA Modules:
  0.0 86.5 jit_solution(5831722143107814475)
XLA Ops:
  0.6 2.1 %keyval.1 = bf16[8,128,128]{2,1,0:T(8,128)(2,1)} custom-call(s32[8]{0:T(128)} %bitcast.40, bf16[256,1024]{1,0:T(8,128)(2,1)} %bitcast.25, bf16[1024,128]{1,0:T(8,128)(2,1)} %bitcast.37), custom_call_target="tpu_custom_call" | custom-call | tf_op jit(solution)/shard_map/keyval/pallas_call | solution.py:312
  2.8 7.3 %all-to-all-start = ((bf16[8,128,128]{2,1,0:T(8,128)(2,1)}), bf16[8,128,128]{2,1,0:T(8,128)(2,1)S(1)}, u32[]{:S(2)}, u32[]{:S(2)}) async-start(bf16[8,128,128]{2,1,0:T(8,128)(2,1)} %keyval.1), calls=%async_computation | async-start | bytes 524288 | tf_op jit(solution)/shard_map/all_to_all | solution.py:320
  10.1 3.0 %project.1 = (bf16[4,128,512]{2,1,0:T(8,128)(2,1)}, bf16[2,4,256,128]{3,2,1,0:T(8,128)(2,1)}) custom-call(bf16[256,1024]{1,0:T(8,128)(2,1)} %bitcast.26, bf16[1024,256]{1,0:T(8,128)(2,1)} %bitcast.36, bf16[256,1024]{1,0:T(8,128)(2,1)} %bitcast.30, bf16[256,1024]{1,0:T(8,128)(2,1)} %cot_ref.3), custom_call_target="tpu_custom_call" | custom-call | tf_op jit(solution)/shard_map/project/pallas_call | solution.py:324
  13.1 2.0 %collective-permute-start.3 = (bf16[2,4,256,128]{3,2,1,0:T(8,128)(2,1)}, bf16[2,4,256,128]{3,2,1,0:T(8,128)(2,1)S(1)}, u32[]{:S(2)}, u32[]{:S(2)}) collective-permute-start(bf16[2,4,256,128]{3,2,1,0:T(8,128)(2,1)} %get-tuple-element.18), channel_id=1, source_target_pairs={{0,4},{4,0},{8,12},{12,8},{16,20},{20,16},{24,28},{28,24},{1,5},{5... | collective-permute-start | bytes 1572872 | tf_op jit(solution)/shard_map/ppermute | solution.py:334
  15.1 4.0 %all-to-all-done = bf16[8,128,128]{2,1,0:T(8,128)(2,1)S(1)} async-done(((bf16[8,128,128]{2,1,0:T(8,128)(2,1)}), bf16[8,128,128]{2,1,0:T(8,128)(2,1)S(1)}, u32[]{:S(2)}, u32[]{:S(2)}) %all-to-all-start) | async-done | bytes 262176 | tf_op jit(solution)/shard_map/all_to_all | solution.py:320
  19.1 0.7 copy-done.1
  19.8 7.9 %attention.1 = (bf16[1024,128]{1,0:T(8,128)(2,1)}, bf16[2,4,64,256]{3,2,1,0:T(8,128)(2,1)}) custom-call(bf16[4,128,512]{2,1,0:T(8,128)(2,1)} %get-tuple-element.14.w_ref, bf16[1024,128]{1,0:T(8,128)(2,1)} %bitcast.32), custom_call_target="tpu_custom_call" | custom-call | tf_op jit(solution)/shard_map/attention/pallas_call | solution.py:335
  27.7 2.5 %output.1 = (f32[2,64,1024]{2,1,0:T(8,128)}, f32[2,64,1024]{2,1,0:T(8,128)}) custom-call(bf16[2,256,256]{2,1,0:T(8,128)(2,1)} %bitcast.33, bf16[256,1024]{1,0:T(8,128)(2,1)} %bitcast.31), custom_call_target="tpu_custom_call" | custom-call | tf_op jit(solution)/shard_map/output/pallas_call | solution.py:351
  30.2 0.0 collective-permute-start
  30.2 3.6 %all-to-all-start.1 = ((bf16[8,128,128]{2,1,0:T(8,128)(2,1)}), bf16[8,128,128]{2,1,0:T(8,128)(2,1)S(1)}, u32[]{:S(2)}, u32[]{:S(2)}) async-start(bf16[8,128,128]{2,1,0:T(8,128)(2,1)} %bitcast.13), calls=%async_computation.1 | async-start | bytes 524288 | tf_op jit(solution)/shard_map/all_to_all | solution.py:346
  33.8 0.0 copy-done.2
  33.9 2.0 %collective-permute-start.2 = (bf16[2,256,256]{2,1,0:T(8,128)(2,1)S(1)}, bf16[2,256,256]{2,1,0:T(8,128)(2,1)S(1)}, u32[]{:S(2)}, u32[]{:S(2)}) collective-permute-start(bf16[2,256,256]{2,1,0:T(8,128)(2,1)S(1)} %bitcast.35), channel_id=1, source_target_pairs={{0,4},{4,0},{8,12},{12,8},{16,20},{20,16},{24,28},{28,24},{1,5},{5... | collective-permute-start | bytes 786440 | tf_op jit(solution)/shard_map/ppermute | solution.py:350
  35.9 0.0 collective-permute-done.3.half_ref
  35.9 9.5 %collective-permute-done.2.mix_got_ref = bf16[2,256,256]{2,1,0:T(8,128)(2,1)S(1)} collective-permute-done((bf16[2,256,256]{2,1,0:T(8,128)(2,1)S(1)}, bf16[2,256,256]{2,1,0:T(8,128)(2,1)S(1)}, u32[]{:S(2)}, u32[]{:S(2)}) %collective-permute-start.2) | collective-permute-done | bytes 262176 | tf_op jit(solution)/shard_map/ppermute | solution.py:350
  45.4 0.0 copy-done.4
  45.4 0.7 copy-done.8
  46.1 3.3 %weights.1 = (f32[512,128]{1,0:T(8,128)}, f32[528,128]{1,0:T(8,128)}, f32[528,128]{1,0:T(8,128)}, f32[528,128]{1,0:T(8,128)}) custom-call(bf16[2,256,256]{2,1,0:T(8,128)(2,1)} %bitcast.34, bf16[2,256,256]{2,1,0:T(8,128)(2,1)} %copy-done.8, bf16[256,1024]{1,0:T(8,128)(2,1)} %cot_ref.3, bf16[256,1024]{1,0:T(8,128)(2,1)} %bitcast.27, ...), custom_call_target="tpu_custom_call" | custom-call | tf_op jit(solution)/shard_map/weights/pallas_call | solution.py:362
  49.4 1.0 %convert_element_type.50 = f16[528,128]{1,0:T(8,128)(2,1)S(1)} convert(f32[528,128]{1,0:T(8,128)} %get-tuple-element.22) | non-fusion elementwise | flops 67584 | bytes 405504 | tf_op jit(solution)/shard_map/convert_element_type | solution.py:374
  50.4 0.0 copy-start.5
  50.4 3.4 %collective-permute-start.6 = (f16[528,128]{1,0:T(8,128)(2,1)S(1)}, f16[528,128]{1,0:T(8,128)(2,1)S(1)}, u32[]{:S(2)}, u32[]{:S(2)}) collective-permute-start(f16[528,128]{1,0:T(8,128)(2,1)S(1)} %convert_element_type.50), channel_id=1, source_target_pairs={{0,24},{4,28},{8,16},{12,20},{16,8},{20,12},{24,0},{28,4},{1,25},{... | collective-permute-start | bytes 405512 | tf_op jit(solution)/shard_map/ppermute | solution.py:375
  53.8 0.0 copy-done.6
  53.8 0.1 collective-permute-start.5
  53.9 0.0 copy-done.5
  53.9 1.1 %collective-permute-start.4 = (f16[528,128]{1,0:T(8,128)(2,1)S(1)}, f16[528,128]{1,0:T(8,128)(2,1)S(1)}, u32[]{:S(2)}, u32[]{:S(2)}) collective-permute-start(f16[528,128]{1,0:T(8,128)(2,1)S(1)} %convert_element_type.44), channel_id=1, source_target_pairs={{0,8},{4,12},{8,0},{12,4},{16,24},{20,28},{24,16},{28,20},{1,9},{5... | collective-permute-start | bytes 405512 | tf_op jit(solution)/shard_map/ppermute | solution.py:375
  55.1 3.6 %collective-permute-done.6 = f16[528,128]{1,0:T(8,128)(2,1)S(1)} collective-permute-done((f16[528,128]{1,0:T(8,128)(2,1)S(1)}, f16[528,128]{1,0:T(8,128)(2,1)S(1)}, u32[]{:S(2)}, u32[]{:S(2)}) %collective-permute-start.6) | collective-permute-done | bytes 135200 | tf_op jit(solution)/shard_map/ppermute | solution.py:375
  58.7 0.5 slice.55
  59.9 5.2 %collective-permute-done.5 = f16[528,128]{1,0:T(8,128)(2,1)S(1)} collective-permute-done((f16[528,128]{1,0:T(8,128)(2,1)S(1)}, f16[528,128]{1,0:T(8,128)(2,1)S(1)}, u32[]{:S(2)}, u32[]{:S(2)}) %collective-permute-start.5) | collective-permute-done | bytes 135200 | tf_op jit(solution)/shard_map/ppermute | solution.py:375
  65.1 0.5 slice.53
  66.3 0.0 collective-permute-done.4
  66.4 0.5 slice.51
  67.6 0.0 all-to-all-done.1.ret_ref
  67.6 0.0 copy-start
  67.6 0.7 copy-done
  68.3 2.5 %owner.1 = f32[8,144,128]{2,1,0:T(8,128)} custom-call(s32[8]{0:T(128)} %bitcast.41, bf16[8,128,128]{2,1,0:T(8,128)(2,1)} %copy-done, bf16[256,1024]{1,0:T(8,128)(2,1)} %bitcast.28), custom_call_target="tpu_custom_call" | custom-call | tf_op jit(solution)/shard_map/owner/pallas_call | solution.py:376
  70.8 1.9 %convert_element_type.53 = f16[8,144,128]{2,1,0:T(8,128)(2,1)} convert(f32[8,144,128]{2,1,0:T(8,128)} %owner.1) | non-fusion elementwise | flops 147456 | bytes 884736 | tf_op jit(solution)/shard_map/convert_element_type | solution.py:383
  72.6 4.1 %all-to-all-start.2 = ((f16[8,144,128]{2,1,0:T(8,128)(2,1)}), f16[8,144,128]{2,1,0:T(8,128)(2,1)S(1)}, u32[]{:S(2)}, u32[]{:S(2)}) async-start(f16[8,144,128]{2,1,0:T(8,128)(2,1)} %convert_element_type.53), calls=%async_computation.2 | async-start | bytes 589824 | tf_op jit(solution)/shard_map/all_to_all | solution.py:384
  76.7 0.0 collective-permute-done
  76.7 0.0 copy-done.3
  76.7 0.1 add.22
  76.8 1.6 %collective-permute-start.1 = (f32[64,1024]{1,0:T(8,128)S(1)}, f32[64,1024]{1,0:T(8,128)S(1)}, u32[]{:S(2)}, u32[]{:S(2)}) collective-permute-start(f32[64,1024]{1,0:T(8,128)S(1)} %slice_bitcast_fusion), channel_id=1, source_target_pairs={{0,2},{1,3},{2,0},{3,1},{4,6},{5,7},{6,4},{7,5},{8,10},{9,11},{10,... | collective-permute-start | bytes 786440 | tf_op jit(solution)/shard_map/ppermute | solution.py:386
  78.4 0.0 copy-done.7
  78.4 0.1 multiply_add_fusion
  78.5 0.7 slice_bitcast_fusion.2
  79.2 4.7 %collective-permute-done.1 = f32[64,1024]{1,0:T(8,128)S(1)} collective-permute-done((f32[64,1024]{1,0:T(8,128)S(1)}, f32[64,1024]{1,0:T(8,128)S(1)}, u32[]{:S(2)}, u32[]{:S(2)}) %collective-permute-start.1) | collective-permute-done | bytes 262176 | tf_op jit(solution)/shard_map/ppermute | solution.py:386
  83.9 1.6 %fusion.2 = bf16[64,1024]{1,0:T(8,128)(2,1)} fusion(f32[64,1024]{1,0:T(8,128)S(1)} %collective-permute-done.1, f32[2,64,1024]{2,1,0:T(8,128)S(1)} %add.22, bf16[256,1024]{1,0:T(8,128)(2,1)} %bitcast.29, s32[]{:T(128)S(6)} %select_n.3), kind=kLoop, calls=%fused_computation.5 | loop fusion | flops 262144 | bytes 786436 | tf_op jit(solution)/shard_map/convert_element_type | solution.py:388
  85.5 0.1 all-to-all-done.2
  85.6 0.1 fusion.5
  85.8 0.7 multiply_reduce_fusion
  (10 shorter events, 0.1 us)
Async XLA Ops:
  2.8 16.3 %all-to-all-start = ((bf16[8,128,128]{2,1,0:T(8,128)(2,1)}), bf16[8,128,128]{2,1,0:T(8,128)(2,1)S(1)}, u32[]{:S(2)}, u32[]{:S(2)}) async-start(bf16[8,128,128]{2,1,0:T(8,128)(2,1)} %keyval.1), calls=%async_computation | async-start | bytes 524288 | tf_op jit(solution)/shard_map/all_to_all | solution.py:320
  13.1 22.8 %collective-permute-start.3 = (bf16[2,4,256,128]{3,2,1,0:T(8,128)(2,1)}, bf16[2,4,256,128]{3,2,1,0:T(8,128)(2,1)S(1)}, u32[]{:S(2)}, u32[]{:S(2)}) collective-permute-start(bf16[2,4,256,128]{3,2,1,0:T(8,128)(2,1)} %get-tuple-element.18), channel_id=1, source_target_pairs={{0,4},{4,0},{8,12},{12,8},{16,20},{20,16},{24,28},{28,24},{1,5},{5... | collective-permute-start | bytes 1572872 | tf_op jit(solution)/shard_map/ppermute | solution.py:334
  19.1 0.7 copy-start.1
  30.2 46.5 %collective-permute-start = (f32[2,64,1024]{2,1,0:T(8,128)}, f32[2,64,1024]{2,1,0:T(8,128)S(1)}, u32[]{:S(2)}, u32[]{:S(2)}) collective-permute-start(f32[2,64,1024]{2,1,0:T(8,128)} %get-tuple-element.17), channel_id=1, source_target_pairs={{0,1},{1,0},{2,3},{3,2},{4,5},{5,4},{6,7},{7,6},{8,9},{9,8},{10,11... | collective-permute-start | bytes 1572872 | tf_op jit(solution)/shard_map/ppermute | solution.py:361
  30.2 3.6 %copy-start.2 = (bf16[2,4,64,256]{3,2,1,0:T(8,128)(2,1)S(1)}, bf16[2,4,64,256]{3,2,1,0:T(8,128)(2,1)}, u32[]{:S(2)}) copy-start(bf16[2,4,64,256]{3,2,1,0:T(8,128)(2,1)} %get-tuple-element.15) | copy-start | bytes 786436
  30.2 37.3 %all-to-all-start.1 = ((bf16[8,128,128]{2,1,0:T(8,128)(2,1)}), bf16[8,128,128]{2,1,0:T(8,128)(2,1)S(1)}, u32[]{:S(2)}, u32[]{:S(2)}) async-start(bf16[8,128,128]{2,1,0:T(8,128)(2,1)} %bitcast.13), calls=%async_computation.1 | async-start | bytes 524288 | tf_op jit(solution)/shard_map/all_to_all | solution.py:346
  33.9 11.6 %collective-permute-start.2 = (bf16[2,256,256]{2,1,0:T(8,128)(2,1)S(1)}, bf16[2,256,256]{2,1,0:T(8,128)(2,1)S(1)}, u32[]{:S(2)}, u32[]{:S(2)}) collective-permute-start(bf16[2,256,256]{2,1,0:T(8,128)(2,1)S(1)} %bitcast.35), channel_id=1, source_target_pairs={{0,4},{4,0},{8,12},{12,8},{16,20},{20,16},{24,28},{28,24},{1,5},{5... | collective-permute-start | bytes 786440 | tf_op jit(solution)/shard_map/ppermute | solution.py:350
  35.9 9.5 %copy-start.4 = (bf16[2,4,256,128]{3,2,1,0:T(8,128)(2,1)}, bf16[2,4,256,128]{3,2,1,0:T(8,128)(2,1)S(1)}, u32[]{:S(2)}) copy-start(bf16[2,4,256,128]{3,2,1,0:T(8,128)(2,1)S(1)} %collective-permute-done.3.half_ref) | copy-start | bytes 1572868
  45.4 0.7 copy-start.8
  49.4 4.4 %copy-start.6 = (f32[528,128]{1,0:T(8,128)S(1)}, f32[528,128]{1,0:T(8,128)}, u32[]{:S(2)}) copy-start(f32[528,128]{1,0:T(8,128)} %get-tuple-element.21) | copy-start | bytes 811012
  50.4 3.5 %copy-start.5 = (f32[528,128]{1,0:T(8,128)S(1)}, f32[528,128]{1,0:T(8,128)}, u32[]{:S(2)}) copy-start(f32[528,128]{1,0:T(8,128)} %get-tuple-element.20) | copy-start | bytes 811012
  50.4 8.3 %collective-permute-start.6 = (f16[528,128]{1,0:T(8,128)(2,1)S(1)}, f16[528,128]{1,0:T(8,128)(2,1)S(1)}, u32[]{:S(2)}, u32[]{:S(2)}) collective-permute-start(f16[528,128]{1,0:T(8,128)(2,1)S(1)} %convert_element_type.50), channel_id=1, source_target_pairs={{0,24},{4,28},{8,16},{12,20},{16,8},{20,12},{24,0},{28,4},{1,25},{... | collective-permute-start | bytes 405512 | tf_op jit(solution)/shard_map/ppermute | solution.py:375
  53.8 11.3 %collective-permute-start.5 = (f16[528,128]{1,0:T(8,128)(2,1)S(1)}, f16[528,128]{1,0:T(8,128)(2,1)S(1)}, u32[]{:S(2)}, u32[]{:S(2)}) collective-permute-start(f16[528,128]{1,0:T(8,128)(2,1)S(1)} %convert_element_type.47), channel_id=1, source_target_pairs={{0,16},{4,20},{8,24},{12,28},{16,0},{20,4},{24,8},{28,12},{1,17},{... | collective-permute-start | bytes 405512 | tf_op jit(solution)/shard_map/ppermute | solution.py:375
  53.9 12.4 %collective-permute-start.4 = (f16[528,128]{1,0:T(8,128)(2,1)S(1)}, f16[528,128]{1,0:T(8,128)(2,1)S(1)}, u32[]{:S(2)}, u32[]{:S(2)}) collective-permute-start(f16[528,128]{1,0:T(8,128)(2,1)S(1)} %convert_element_type.44), channel_id=1, source_target_pairs={{0,8},{4,12},{8,0},{12,4},{16,24},{20,28},{24,16},{28,20},{1,9},{5... | collective-permute-start | bytes 405512 | tf_op jit(solution)/shard_map/ppermute | solution.py:375
  67.6 0.7 copy-start
  70.8 6.0 %copy-start.3 = (f32[2,64,1024]{2,1,0:T(8,128)S(1)}, f32[2,64,1024]{2,1,0:T(8,128)}, u32[]{:S(2)}) copy-start(f32[2,64,1024]{2,1,0:T(8,128)} %get-tuple-element.16) | copy-start | bytes 1572868
  72.6 13.0 %all-to-all-start.2 = ((f16[8,144,128]{2,1,0:T(8,128)(2,1)}), f16[8,144,128]{2,1,0:T(8,128)(2,1)S(1)}, u32[]{:S(2)}, u32[]{:S(2)}) async-start(f16[8,144,128]{2,1,0:T(8,128)(2,1)} %convert_element_type.53), calls=%async_computation.2 | async-start | bytes 589824 | tf_op jit(solution)/shard_map/all_to_all | solution.py:384
  76.8 1.6 %copy-start.7 = (f32[512,128]{1,0:T(8,128)S(1)}, f32[512,128]{1,0:T(8,128)}, u32[]{:S(2)}) copy-start(f32[512,128]{1,0:T(8,128)} %get-tuple-element.19) | copy-start | bytes 786436
  76.8 7.1 %collective-permute-start.1 = (f32[64,1024]{1,0:T(8,128)S(1)}, f32[64,1024]{1,0:T(8,128)S(1)}, u32[]{:S(2)}, u32[]{:S(2)}) collective-permute-start(f32[64,1024]{1,0:T(8,128)S(1)} %slice_bitcast_fusion), channel_id=1, source_target_pairs={{0,2},{1,3},{2,0},{3,1},{4,6},{5,7},{6,4},{7,5},{8,10},{9,11},{10,... | collective-permute-start | bytes 786440 | tf_op jit(solution)/shard_map/ppermute | solution.py:386
where the time goes:
time: 87.2 us; the launch traced here: 86.5 us
  waiting for transfers between devices  27.2 us (31%)
  starting transfers between devices  25.2 us (29%)
  Pallas kernels  21.3 us (24%)
  other arithmetic  5.58 us (6%)
  local copies, waits for them, and re-layouts  4.4 us (5%)
  between operations  2.85 us (3%)
    ppermute x1, waiting for transfers between devices, shared_local(): mix_got = lax.ppermute(mix, 'graph', xor_pairs(parts, 1))  9.53 us
    ppermute x3, waiting for transfers between devices, shared_local(): sums_got.append(lax.ppermute(away, 'graph', xor_pairs(parts, 2 * d)))  8.86 us
    pallas_call x1, Pallas kernels, shared_local(): pl.pallas_call(attention_kernel, out_shape=(jax.ShapeDtypeStruct((keys, k...  7.93 us
    all_to_all x1, starting transfers between devices, shared_local(): lax.all_to_all(outgoing, 'graph', split_axis=0, concat_axis=0, tiled=True)  7.31 us
    ppermute x1, waiting for transfers between devices, shared_local(): out_last = lax.ppermute(out_half[1], 'mp', xor_pairs(mp, 2))  4.7 us
    ppermute x3, starting transfers between devices, shared_local(): sums_got.append(lax.ppermute(away, 'graph', xor_pairs(parts, 2 * d)))  4.56 us
    all_to_all x1, starting transfers between devices, shared_local(): lax.all_to_all(kv_parts, 'graph', split_axis=0, concat_axis=0, tiled=True)  4.07 us
    all_to_all x1, waiting for transfers between devices, shared_local(): lax.all_to_all(outgoing, 'graph', split_axis=0, concat_axis=0, tiled=True)  3.98 us
  transfers between devices with their start and end apart: 10, of which 6 were waited for; matrix products, arithmetic and copies ran while one was open for 8% of the time, Pallas kernels for 22%

commit v1 on v0

--- a/solution.py
+++ b/solution.py
@@ -147,16 +147,38 @@
 NT = ((1,), (1,))
 
 
-def keyval_kernel(send_ref, x_ref, wkv_ref, out_ref, kv_ref):
+def keyval_kernel(send_hbm, x_hbm, wkv_hbm, out_ref, x_ref, wkv_ref, send_ref, kv_ref, sems):
     rows = out_ref.shape[1]
-    kv = dot(x_ref[...], wkv_ref[...]).astype(BF16)
+    chunks = sems.shape[1]
+    depth = x_ref.shape[1] // chunks
+    copies = []
+    for c in range(chunks):
+        at = pl.ds(c * depth, depth)
+        pair = (
+            pltpu.make_async_copy(x_hbm.at[:, at], x_ref.at[:, at], sems.at[0, c]),
+            pltpu.make_async_copy(wkv_hbm.at[at], wkv_ref.at[at], sems.at[1, c]),
+        )
+        for copy in pair:
+            copy.start()
+        copies.append(pair)
+    listing = pltpu.make_async_copy(send_hbm, send_ref, sems.at[2, 0])
+    listing.start()
+    kv = None
+    for c, pair in enumerate(copies):
+        for copy in pair:
+            copy.wait()
+        at = pl.ds(c * depth, depth)
+        part = dot(x_ref[:, at], wkv_ref[at])
+        kv = part if kv is None else kv + part
+    kv = kv.astype(BF16)
     for t in range(kv_ref.shape[0]):
         kv_ref[t] = kv[t * rows : (t + 1) * rows]
+    listing.wait()
     for r in range(out_ref.shape[0]):
         out_ref[r] = kv_ref[send_ref[r]]
 
 
-def project_kernel(x_ref, wq_ref, wo_ref, cot_ref, w_ref, half_ref):
+def project_kernel(x_ref, wq_ref, wo_ref, cot_ref, w_ref):
     tokens = x_ref.shape[0]
     groups = w_ref.shape[0]
     query = (dot(x_ref[...], wq_ref[...]) * DH ** (-0.5)).astype(BF16)
@@ -166,6 +188,9 @@
     for k in range(groups):
         w_ref[k, :DH, :tokens] = query_t[k * DH : (k + 1) * DH]
         w_ref[k, DH:, tokens:] = grad_mixed_t[k * DH : (k + 1) * DH]
+
+
+def halves_kernel(cot_ref, x_ref, half_ref):
     other = 1 - lax.rem(lax.axis_index("graph"), 2)
     outer = half_ref.shape[1]
     cols = half_ref.shape[3]
@@ -175,32 +200,39 @@
         half_ref[1, d] = x_ref[:, at]
 
 
-def attention_kernel(w_ref, kv_ref, slot_ref, mix_ref, acc_ref):
+def attention_kernel(w_ref, kv_ref, slot_ref, mix_ref, acc_ref, both_ref, pair_ref):
     groups, _, twice = w_ref.shape
     tokens = twice // 2
     scale = DH ** (-0.5)
-    kv = kv_ref[...]
-    kv_t = kv.T
-    acc_ref[...] = jnp.zeros_like(acc_ref)
-
-    def group(k, carry):
-        weights = w_ref[k]
-        both = dot(kv, weights)
-        score, grad_prob = both[:, :tokens], both[:, tokens:]
-        exponent = jnp.exp(score - jnp.max(score, axis=0, keepdims=True))
-        prob = exponent * (1.0 / jnp.sum(exponent, axis=0, keepdims=True))
+    kv_t = kv_ref[...].T
+
+    def scores(k):
+        both = dot(kv_ref[...], w_ref[k])
+        both_ref[k % 2] = both
+        return jnp.max(both[:, :tokens], axis=0, keepdims=True)
+
+    top = scores(0)
+    for k in range(groups):
+        b = k % 2
+        exponent = jnp.exp(both_ref[b, :, :tokens] - top)
+        grad_prob = both_ref[b, :, tokens:]
+        inverse = 1.0 / jnp.sum(exponent, axis=0, keepdims=True)
+        prob = exponent * inverse
         delta = jnp.sum(prob * grad_prob, axis=0, keepdims=True)
-        rounded = prob.astype(BF16)
-        grad_score = (prob * (grad_prob - delta)).astype(BF16)
-        pair = jnp.concatenate([grad_score, rounded], axis=1)
-        outs = dot(kv_t, pair)
+        pair_ref[b, :, tokens:] = prob.astype(BF16)
+        pair_ref[b, :, :tokens] = (prob * (grad_prob - delta)).astype(BF16)
+        if k + 1 < groups:
+            top = scores(k + 1)
+        outs = dot(kv_t, pair_ref[b])
         mix_ref[0, k] = outs[DH:, tokens:].astype(BF16)
         mix_ref[1, k] = (outs[:DH, :tokens] * scale).astype(BF16)
-        acc_ref[...] += dot(pair, weights, NT)
-        return carry
-
-    lax.fori_loop(0, groups, group, 0)
-    slot_ref[...] = acc_ref[...].astype(BF16)
+        grad = dot(pair_ref[b], w_ref[k], NT)
+        if k == 0:
+            acc_ref[...] = grad
+        elif k + 1 < groups:
+            acc_ref[...] += grad
+        else:
+            slot_ref[...] = (acc_ref[...] + grad).astype(BF16)
 
 
 def output_kernel(mix_ref, wo_ref, out_keep_ref, out_send_ref):
@@ -279,9 +311,30 @@
         out_ref[r, kv_width:] = jnp.broadcast_to(e, out_ref[r, kv_width:].shape)
 
 
-def unscaled(got):
-    rows = got.shape[-2] - 16
-    return got[..., :rows, :].astype(F32) * jnp.exp2(got[..., rows : rows + 1, :1].astype(F32))
+def unscaled(value):
+    rows = value.shape[0] - 16
+    return value[:rows] * jnp.exp2(value[rows : rows + 1])
+
+
+def sums_kernel(own_ref, *refs):
+    *got_refs, wo_ref, wq_ref = refs
+    total = own_ref[...]
+    for ref in got_refs:
+        total = total + unscaled(ref[...])
+    half = wo_ref.shape[0]
+    wo_ref[...] = total[:half]
+    wq_ref[...] = total[half:]
+
+
+def kvsum_kernel(got_ref, out_ref):
+    total = unscaled(got_ref[0])
+    for r in range(1, got_ref.shape[0]):
+        total = total + unscaled(got_ref[r])
+    out_ref[...] = total
+
+
+GRANT = pltpu.CompilerParams(vmem_limit_bytes=8 << 20)
+WIDE = pltpu.CompilerParams(vmem_limit_bytes=16 << 20)
 
 
 def vmem(count):
@@ -312,25 +365,37 @@
     outgoing = pl.pallas_call(
         keyval_kernel,
         out_shape=jax.ShapeDtypeStruct((parts, rows, kv_width), BF16),
-        in_specs=[SMEM] + vmem(2),
+        in_specs=[pl.BlockSpec(memory_space=pltpu.HBM)] * 3,
         out_specs=vmem(1)[0],
-        scratch_shapes=[pltpu.VMEM((tiles, rows, kv_width), BF16)],
+        scratch_shapes=[
+            pltpu.VMEM(x.shape, BF16),
+            pltpu.VMEM(wkv2.shape, BF16),
+            pltpu.SMEM(send.shape, jnp.int32),
+            pltpu.VMEM((tiles, rows, kv_width), BF16),
+            pltpu.SemaphoreType.DMA((3, 4)),
+        ],
         name="keyval",
     )(send, x, wkv2)
     received = lax.all_to_all(outgoing, "graph", split_axis=0, concat_axis=0, tiled=True)
     keys = parts * rows
     share = tokens // mp
     outer = parts // 2
-    weights, half = pl.pallas_call(
+    weights = pl.pallas_call(
         project_kernel,
-        out_shape=(
-            jax.ShapeDtypeStruct((groups, kv_width, 2 * tokens), BF16),
-            jax.ShapeDtypeStruct((2, outer, tokens, cols), BF16),
-        ),
+        out_shape=jax.ShapeDtypeStruct((groups, kv_width, 2 * tokens), BF16),
         in_specs=vmem(4),
-        out_specs=tuple(vmem(2)),
+        out_specs=vmem(1)[0],
+        compiler_params=GRANT,
         name="project",
     )(x, wq2, wo2, cotangent)
+    half = pl.pallas_call(
+        halves_kernel,
+        out_shape=jax.ShapeDtypeStruct((2, outer, tokens, cols), BF16),
+        in_specs=vmem(2),
+        out_specs=vmem(1)[0],
+        compiler_params=GRANT,
+        name="halves",
+    )(cotangent, x)
     half_got = lax.ppermute(half, "graph", xor_pairs(parts, 1))
     slot_grad, mix = pl.pallas_call(
         attention_kernel,
@@ -340,7 +405,12 @@
         ),
         in_specs=vmem(2),
         out_specs=tuple(vmem(2)),
-        scratch_shapes=[pltpu.VMEM((keys, kv_width), F32)],
+        scratch_shapes=[
+            pltpu.VMEM((keys, kv_width), F32),
+            pltpu.VMEM((2, keys, 2 * tokens), F32),
+            pltpu.VMEM((2, keys, 2 * tokens), BF16),
+        ],
+        compiler_params=WIDE,
         name="attention",
     )(weights, received.reshape(keys, kv_width))
     returned = lax.all_to_all(
@@ -356,6 +426,7 @@
         ),
         in_specs=vmem(2),
         out_specs=tuple(vmem(2)),
+        compiler_params=GRANT,
         name="output",
     )(mix, wo2)
     out_got = lax.ppermute(out_away, "mp", xor_pairs(mp, 1))
@@ -367,6 +438,7 @@
         ),
         in_specs=vmem(5),
         out_specs=tuple(vmem(outer)),
+        compiler_params=GRANT,
         name="weights",
     )(mix, mix_got, cotangent, x, half_got)
     sums_got = []
@@ -378,6 +450,7 @@
         out_shape=jax.ShapeDtypeStruct((parts, kv_width + 16, cols), F32),
         in_specs=[SMEM] + vmem(2),
         out_specs=vmem(1)[0],
+        compiler_params=GRANT,
         name="owner",
     )(send, returned, x)
     kv_parts = kv_parts.astype(jnp.float16)
@@ -386,10 +459,22 @@
     out_last = lax.ppermute(out_half[1], "mp", xor_pairs(mp, 2))
     own_rows = lax.dynamic_slice_in_dim(x, lax.axis_index("mp") * share, share, 0)
     output = (own_rows.astype(F32) + (out_half[0] + out_last)).astype(BF16)
-    for got in sums_got:
-        sums = sums + unscaled(got)
-    grad_wo, grad_wq = sums[:head_width], sums[head_width:]
-    grad_wkv = jnp.sum(unscaled(kv_got), axis=0)
+    grad_wo, grad_wq = pl.pallas_call(
+        sums_kernel,
+        out_shape=tuple(jax.ShapeDtypeStruct((head_width, cols), F32) for _ in range(2)),
+        in_specs=vmem(outer),
+        out_specs=tuple(vmem(2)),
+        compiler_params=GRANT,
+        name="sums",
+    )(sums, *(got.astype(F32) for got in sums_got))
+    grad_wkv = pl.pallas_call(
+        kvsum_kernel,
+        out_shape=jax.ShapeDtypeStruct((kv_width, cols), F32),
+        in_specs=vmem(1),
+        out_specs=vmem(1)[0],
+        compiler_params=GRANT,
+        name="kvsum",
+    )(kv_got.astype(F32))
     return (
         output,
         grad_wq.reshape(cols, *wq.shape[1:]),

time: 87.2 us -> 75.2 us (0.86)
  Pallas kernels: 21.3 us -> 13.7 us
  waiting for transfers between devices: 27.2 us -> 32.6 us
  local copies, waits for them, and re-layouts: 4.4 us -> 1.44 us
  other arithmetic: 5.58 us -> 2.67 us
  between operations: 2.85 us -> 0.82 us
  starting transfers between devices: 25.2 us -> 23.3 us
    all_to_all x1, waiting for transfers between devices: 0.01 us -> 7.43 us  [shared_local(): lax.all_to_all(slot_grad.reshape(parts, rows, kv_width), 'graph', split_a...]
    ppermute x1, waiting for transfers between devices: 4.7 us -> 0.01 us  [shared_local(): out_last = lax.ppermute(out_half[1], 'mp', xor_pairs(mp, 2))]
    all_to_all x1, waiting for transfers between devices: 3.98 us -> 7.36 us  [shared_local(): lax.all_to_all(outgoing, 'graph', split_axis=0, concat_axis=0, tiled=True)]
    pallas_call x1, Pallas kernels: 7.93 us -> 4.94 us  [shared_local(): pl.pallas_call(attention_kernel, out_shape=(jax.ShapeDtypeStruct((keys, k...]
    ppermute x1, waiting for transfers between devices: 9.53 us -> 7.54 us  [shared_local(): mix_got = lax.ppermute(mix, 'graph', xor_pairs(parts, 1))]
    ppermute x1, starting transfers between devices: 2.02 us -> 0.08 us  [shared_local(): mix_got = lax.ppermute(mix, 'graph', xor_pairs(parts, 1))]
    slice x3 -> x0, local copies, waits for them, and re-layouts: 1.54 us -> none  [unscaled(): got[..., rows:rows + 1, :1].astype(F32)]
    pallas_call x1, Pallas kernels: 2.47 us -> 1.06 us  [shared_local(): pl.pallas_call(owner_kernel, out_shape=jax.ShapeDtypeStruct((parts, kv_wi...]
  transfers between devices with their start and end apart: 10 -> 10, of which waited for: 6 -> 6; matrix products, arithmetic and copies ran while one was open for 8% -> 2% of each run, Pallas kernels for 22% -> 6%
where the time goes in v1:
time: 75.2 us; the launch traced here: 74.5 us
  waiting for transfers between devices  32.6 us (43%)
  starting transfers between devices  23.3 us (31%)
  Pallas kernels  13.7 us (18%)
  other arithmetic  2.67 us (4%)
  local copies, waits for them, and re-layouts  1.44 us (2%)
  between operations  0.82 us (1%)
    ppermute x3, waiting for transfers between devices, shared_local(): sums_got.append(lax.ppermute(away, 'graph', xor_pairs(parts, 2 * d)))  9.64 us
    ppermute x1, waiting for transfers between devices, shared_local(): mix_got = lax.ppermute(mix, 'graph', xor_pairs(parts, 1))  7.54 us
    all_to_all x1, starting transfers between devices, shared_local(): lax.all_to_all(outgoing, 'graph', split_axis=0, concat_axis=0, tiled=True)  7.45 us
    all_to_all x1, waiting for transfers between devices, shared_local(): lax.all_to_all(slot_grad.reshape(parts, rows, kv_width), 'graph', split_a...  7.43 us
    all_to_all x1, waiting for transfers between devices, shared_local(): lax.all_to_all(outgoing, 'graph', split_axis=0, concat_axis=0, tiled=True)  7.36 us
    pallas_call x1, Pallas kernels, shared_local(): pl.pallas_call(attention_kernel, out_shape=(jax.ShapeDtypeStruct((keys, k...  4.94 us
    ppermute x3, starting transfers between devices, shared_local(): sums_got.append(lax.ppermute(away, 'graph', xor_pairs(parts, 2 * d)))  4.52 us
    all_to_all x1, starting transfers between devices, shared_local(): lax.all_to_all(kv_parts, 'graph', split_axis=0, concat_axis=0, tiled=True)  4.06 us
  transfers between devices with their start and end apart: 10, of which 6 were waited for; matrix products, arithmetic and copies ran while one was open for 2% of the time, Pallas kernels for 6%

profile of v1, /device:TPU:0, one launch (start us, length us, event | category | flops | bytes accessed | tf_op | source)
XLA Modules:
  0.0 74.5 jit_solution(4524870136451031161)
XLA Ops:
  0.6 0.0 copy-start.1
  0.6 0.0 copy-start.2
  0.7 2.5 %keyval.1 = bf16[8,128,128]{2,1,0:T(8,128)(2,1)} custom-call(s32[8]{0:T(128)} %bitcast.36, bf16[256,1024]{1,0:T(8,128)(2,1)} %bitcast.23, bf16[1024,128]{1,0:T(8,128)(2,1)} %bitcast.38), custom_call_target="tpu_custom_call" | custom-call | tf_op jit(solution)/shard_map/keyval/pallas_call | solution.py:365
  3.2 0.0 copy-start
  3.2 7.5 %all-to-all-start = ((bf16[8,128,128]{2,1,0:T(8,128)(2,1)}), bf16[8,128,128]{2,1,0:T(8,128)(2,1)S(1)}, u32[]{:S(2)}, u32[]{:S(2)}) async-start(bf16[8,128,128]{2,1,0:T(8,128)(2,1)} %keyval.1), calls=%async_computation | async-start | bytes 524288 | tf_op jit(solution)/shard_map/all_to_all | solution.py:379
  10.7 0.0 copy-done.1
  10.7 0.0 copy-done.2
  10.7 0.0 copy-done
  10.7 0.0 copy-start.3
  10.7 1.0 %copy-done.3 = bf16[1024,1,256]{2,0,1:T(8,128)(2,1)S(1)} copy-done((bf16[1024,1,256]{2,0,1:T(8,128)(2,1)S(1)}, bf16[1024,1,256]{2,0,1:T(8,128)(2,1)}, u32[]{:S(2)}) %copy-start.3) | copy-done | bytes 524312
  11.7 0.5 project.1.w_ref
  12.2 7.4 %all-to-all-done = bf16[8,128,128]{2,1,0:T(8,128)(2,1)S(1)} async-done(((bf16[8,128,128]{2,1,0:T(8,128)(2,1)}), bf16[8,128,128]{2,1,0:T(8,128)(2,1)S(1)}, u32[]{:S(2)}, u32[]{:S(2)}) %all-to-all-start) | async-done | bytes 262176 | tf_op jit(solution)/shard_map/all_to_all | solution.py:379
  19.6 4.9 %attention.1 = (bf16[1024,128]{1,0:T(8,128)(2,1)}, bf16[2,4,64,256]{3,2,1,0:T(8,128)(2,1)S(1)}) custom-call(bf16[4,128,512]{2,1,0:T(8,128)(2,1)S(1)} %project.1.w_ref, bf16[1024,128]{1,0:T(8,128)(2,1)S(1)} %bitcast.31), custom_call_target="tpu_custom_call" | custom-call | tf_op jit(solution)/shard_map/attention/pallas_call | solution.py:400
  24.5 1.2 %output.1 = (f32[2,64,1024]{2,1,0:T(8,128)S(1)}, f32[2,64,1024]{2,1,0:T(8,128)}) custom-call(bf16[2,256,256]{2,1,0:T(8,128)(2,1)S(1)} %bitcast.32, bf16[256,1024]{1,0:T(8,128)(2,1)S(1)} %bitcast.30), custom_call_target="tpu_custom_call" | custom-call | tf_op jit(solution)/shard_map/output/pallas_call | solution.py:421
  25.7 0.0 collective-permute-start
  25.7 3.6 %all-to-all-start.1 = ((bf16[8,128,128]{2,1,0:T(8,128)(2,1)}), bf16[8,128,128]{2,1,0:T(8,128)(2,1)S(1)}, u32[]{:S(2)}, u32[]{:S(2)}) async-start(bf16[8,128,128]{2,1,0:T(8,128)(2,1)} %bitcast.10), calls=%async_computation.1 | async-start | bytes 524288 | tf_op jit(solution)/shard_map/all_to_all | solution.py:416
  29.3 0.0 copy-start.4
  29.3 0.2 halves.1
  29.5 2.1 %collective-permute-start.3 = (bf16[2,4,256,128]{3,2,1,0:T(8,128)(2,1)S(1)}, bf16[2,4,256,128]{3,2,1,0:T(8,128)(2,1)}, u32[]{:S(2)}, u32[]{:S(2)}) collective-permute-start(bf16[2,4,256,128]{3,2,1,0:T(8,128)(2,1)S(1)} %halves.1), channel_id=1, source_target_pairs={{0,4},{4,0},{8,12},{12,8},{16,20},{20,16},{24,28},{28,24},{1,5},{5... | collective-permute-start | bytes 1572872 | tf_op jit(solution)/shard_map/ppermute | solution.py:399
  31.5 0.1 collective-permute-start.2
  31.6 7.4 %all-to-all-done.1.ret_ref = bf16[8,128,128]{2,1,0:T(8,128)(2,1)S(1)} async-done(((bf16[8,128,128]{2,1,0:T(8,128)(2,1)}), bf16[8,128,128]{2,1,0:T(8,128)(2,1)S(1)}, u32[]{:S(2)}, u32[]{:S(2)}) %all-to-all-start.1) | async-done | bytes 262176 | tf_op jit(solution)/shard_map/all_to_all | solution.py:416
  39.0 0.0 copy-done.4
  39.0 1.1 %owner.1 = f32[8,144,128]{2,1,0:T(8,128)S(1)} custom-call(s32[8]{0:T(128)S(1)} %bitcast.37, bf16[8,128,128]{2,1,0:T(8,128)(2,1)S(1)} %all-to-all-done.1.ret_ref, bf16[256,1024]{1,0:T(8,128)(2,1)S(1)} %bitcast.26), custom_call_target="tpu_custom_call" | custom-call | tf_op jit(solution)/shard_map/owner/pallas_call | solution.py:448
  40.1 0.8 %convert_element_type.38 = f16[8,144,128]{2,1,0:T(8,128)(2,1)} convert(f32[8,144,128]{2,1,0:T(8,128)S(1)} %owner.1) | non-fusion elementwise | flops 147456 | bytes 884736 | tf_op jit(solution)/shard_map/convert_element_type | solution.py:456
  40.9 4.1 %all-to-all-start.2 = ((f16[8,144,128]{2,1,0:T(8,128)(2,1)}), f16[8,144,128]{2,1,0:T(8,128)(2,1)}, u32[]{:S(2)}, u32[]{:S(2)}) async-start(f16[8,144,128]{2,1,0:T(8,128)(2,1)} %convert_element_type.38), calls=%async_computation.2 | async-start | bytes 589824 | tf_op jit(solution)/shard_map/all_to_all | solution.py:457
  44.9 0.0 collective-permute-done
  44.9 0.1 add.13
  45.0 0.0 copy-start.5
  45.1 1.6 %collective-permute-start.1 = (f32[64,1024]{1,0:T(8,128)S(1)}, f32[64,1024]{1,0:T(8,128)S(1)}, u32[]{:S(2)}, u32[]{:S(2)}) collective-permute-start(f32[64,1024]{1,0:T(8,128)S(1)} %slice_bitcast_fusion), channel_id=1, source_target_pairs={{0,2},{1,3},{2,0},{3,1},{4,6},{5,7},{6,4},{7,5},{8,10},{9,11},{10,... | collective-permute-start | bytes 786440 | tf_op jit(solution)/shard_map/ppermute | solution.py:459
  46.6 0.6 collective-permute-done.3.half_ref
  47.2 0.0 copy-done.5
  47.2 7.5 %collective-permute-done.2.mix_got_ref = bf16[2,256,256]{2,1,0:T(8,128)(2,1)S(1)} collective-permute-done((bf16[2,256,256]{2,1,0:T(8,128)(2,1)S(1)}, bf16[2,256,256]{2,1,0:T(8,128)(2,1)S(1)}, u32[]{:S(2)}, u32[]{:S(2)}) %collective-permute-start.2) | collective-permute-done | bytes 262176 | tf_op jit(solution)/shard_map/ppermute | solution.py:420
  54.8 1.9 %weights.1 = (f32[512,128]{1,0:T(8,128)S(1)}, f32[528,128]{1,0:T(8,128)S(1)}, f32[528,128]{1,0:T(8,128)S(1)}, f32[528,128]{1,0:T(8,128)S(1)}) custom-call(bf16[2,256,256]{2,1,0:T(8,128)(2,1)S(1)} %bitcast.34, bf16[2,256,256]{2,1,0:T(8,128)(2,1)S(1)} %collective-permute-done.2.mix_got_ref, bf16[256,1024]{1,0:T(8,128)(2,1)S(1)} %copy-done.1, ...), custom_call_target="tpu_custom_call" | custom-call | tf_op jit(solution)/shard_map/weights/pallas_call | solution.py:433
  56.7 3.4 %collective-permute-start.6 = (f16[528,128]{1,0:T(8,128)(2,1)S(1)}, f16[528,128]{1,0:T(8,128)(2,1)S(1)}, u32[]{:S(2)}, u32[]{:S(2)}) collective-permute-start(f16[528,128]{1,0:T(8,128)(2,1)S(1)} %convert_element_type.36), channel_id=1, source_target_pairs={{0,24},{4,28},{8,16},{12,20},{16,8},{20,12},{24,0},{28,4},{1,25},{... | collective-permute-start | bytes 405512 | tf_op jit(solution)/shard_map/ppermute | solution.py:447
  60.1 0.0 collective-permute-start.5
  60.1 1.1 %collective-permute-start.4 = (f16[528,128]{1,0:T(8,128)(2,1)S(1)}, f16[528,128]{1,0:T(8,128)(2,1)S(1)}, u32[]{:S(2)}, u32[]{:S(2)}) collective-permute-start(f16[528,128]{1,0:T(8,128)(2,1)S(1)} %convert_element_type.32), channel_id=1, source_target_pairs={{0,8},{4,12},{8,0},{12,4},{16,24},{20,28},{24,16},{28,20},{1,9},{5... | collective-permute-start | bytes 405512 | tf_op jit(solution)/shard_map/ppermute | solution.py:447
  61.3 3.8 %collective-permute-done.6 = f16[528,128]{1,0:T(8,128)(2,1)S(1)} collective-permute-done((f16[528,128]{1,0:T(8,128)(2,1)S(1)}, f16[528,128]{1,0:T(8,128)(2,1)S(1)}, u32[]{:S(2)}, u32[]{:S(2)}) %collective-permute-start.6) | collective-permute-done | bytes 135200 | tf_op jit(solution)/shard_map/ppermute | solution.py:447
  65.1 5.9 %collective-permute-done.5 = f16[528,128]{1,0:T(8,128)(2,1)S(1)} collective-permute-done((f16[528,128]{1,0:T(8,128)(2,1)S(1)}, f16[528,128]{1,0:T(8,128)(2,1)S(1)}, u32[]{:S(2)}, u32[]{:S(2)}) %collective-permute-start.5) | collective-permute-done | bytes 135200 | tf_op jit(solution)/shard_map/ppermute | solution.py:447
  71.0 0.0 collective-permute-done.4
  71.0 0.0 copy-start.6
  71.0 0.8 %sums.1 = (f32[256,128]{1,0:T(8,128)}, f32[256,128]{1,0:T(8,128)}) custom-call(f32[512,128]{1,0:T(8,128)S(1)} %get-tuple-element.17.own_ref, f32[528,128]{1,0:T(8,128)S(1)} %convert_element_type.33.refs_0_, f32[528,128]{1,0:T(8,128)S(1)} %convert_element_type.35.refs_1_, f32[528,128]{1,0:T(8,128)S(1)} %convert_element_type.37.refs_2_), custom_call_target="tpu_custom_call" | custom-call | tf_op jit(solution)/shard_map/sums/pallas_call | solution.py:462
  71.8 0.0 collective-permute-done.1
  71.8 0.4 copy-done.6
  72.1 0.7 fusion.2
  72.9 0.0 all-to-all-done.2
  72.9 1.0 %convert_element_type.39.got_ref = f32[8,144,128]{2,1,0:T(8,128)S(1)} convert(f16[8,144,128]{2,1,0:T(8,128)(2,1)} %all-to-all-done.2) | non-fusion elementwise | flops 147456 | bytes 884736 | tf_op jit(solution)/shard_map/convert_element_type | solution.py:477
  73.9 0.7 kvsum.1
  (7 shorter events, 0.1 us)
Async XLA Ops:
  0.6 10.0 %copy-start.1 = (bf16[256,1024]{1,0:T(8,128)(2,1)S(1)}, bf16[256,1024]{1,0:T(8,128)(2,1)}, u32[]{:S(2)}) copy-start(bf16[256,1024]{1,0:T(8,128)(2,1)} %cot_ref.5) | copy-start | bytes 1572868
  0.6 10.0 %copy-start.2 = (bf16[1,256,1024]{2,1,0:T(8,128)(2,1)S(1)}, bf16[1,256,1024]{2,1,0:T(8,128)(2,1)}, u32[]{:S(2)}) copy-start(bf16[1,256,1024]{2,1,0:T(8,128)(2,1)} %param.10) | copy-start | bytes 1572868
  3.2 7.5 %copy-start = (bf16[2,128,1024]{2,1,0:T(8,128)(2,1)S(1)}, bf16[2,128,1024]{2,1,0:T(8,128)(2,1)}, u32[]{:S(2)}) copy-start(bf16[2,128,1024]{2,1,0:T(8,128)(2,1)} %param.7) | copy-start | bytes 1572868
  3.2 16.4 %all-to-all-start = ((bf16[8,128,128]{2,1,0:T(8,128)(2,1)}), bf16[8,128,128]{2,1,0:T(8,128)(2,1)S(1)}, u32[]{:S(2)}, u32[]{:S(2)}) async-start(bf16[8,128,128]{2,1,0:T(8,128)(2,1)} %keyval.1), calls=%async_computation | async-start | bytes 524288 | tf_op jit(solution)/shard_map/all_to_all | solution.py:379
  10.7 1.0 %copy-start.3 = (bf16[1024,1,256]{2,0,1:T(8,128)(2,1)S(1)}, bf16[1024,1,256]{2,0,1:T(8,128)(2,1)}, u32[]{:S(2)}) copy-start(bf16[1024,1,256]{2,0,1:T(8,128)(2,1)} %param.8) | copy-start | bytes 1572868
  25.7 19.2 %collective-permute-start = (f32[2,64,1024]{2,1,0:T(8,128)}, f32[2,64,1024]{2,1,0:T(8,128)S(1)}, u32[]{:S(2)}, u32[]{:S(2)}) collective-permute-start(f32[2,64,1024]{2,1,0:T(8,128)} %get-tuple-element.16), channel_id=1, source_target_pairs={{0,1},{1,0},{2,3},{3,2},{4,5},{5,4},{6,7},{7,6},{8,9},{9,8},{10,11... | collective-permute-start | bytes 1572872 | tf_op jit(solution)/shard_map/ppermute | solution.py:432
  25.7 13.3 %all-to-all-start.1 = ((bf16[8,128,128]{2,1,0:T(8,128)(2,1)}), bf16[8,128,128]{2,1,0:T(8,128)(2,1)S(1)}, u32[]{:S(2)}, u32[]{:S(2)}) async-start(bf16[8,128,128]{2,1,0:T(8,128)(2,1)} %bitcast.10), calls=%async_computation.1 | async-start | bytes 524288 | tf_op jit(solution)/shard_map/all_to_all | solution.py:416
  29.3 9.7 %copy-start.4 = (s32[1,8,1]{1,2,0:T(1,128)S(1)}, s32[1,8,1]{1,2,0:T(1,128)}, u32[]{:S(2)}) copy-start(s32[1,8,1]{1,2,0:T(1,128)} %param.11) | copy-start | bytes 100
  29.5 17.7 %collective-permute-start.3 = (bf16[2,4,256,128]{3,2,1,0:T(8,128)(2,1)S(1)}, bf16[2,4,256,128]{3,2,1,0:T(8,128)(2,1)}, u32[]{:S(2)}, u32[]{:S(2)}) collective-permute-start(bf16[2,4,256,128]{3,2,1,0:T(8,128)(2,1)S(1)} %halves.1), channel_id=1, source_target_pairs={{0,4},{4,0},{8,12},{12,8},{16,20},{20,16},{24,28},{28,24},{1,5},{5... | collective-permute-start | bytes 1572872 | tf_op jit(solution)/shard_map/ppermute | solution.py:399
  31.5 23.2 %collective-permute-start.2 = (bf16[2,256,256]{2,1,0:T(8,128)(2,1)S(1)}, bf16[2,256,256]{2,1,0:T(8,128)(2,1)S(1)}, u32[]{:S(2)}, u32[]{:S(2)}) collective-permute-start(bf16[2,256,256]{2,1,0:T(8,128)(2,1)S(1)} %bitcast.33), channel_id=1, source_target_pairs={{0,4},{4,0},{8,12},{12,8},{16,20},{20,16},{24,28},{28,24},{1,5},{5... | collective-permute-start | bytes 786440 | tf_op jit(solution)/shard_map/ppermute | solution.py:420
  40.9 32.0 %all-to-all-start.2 = ((f16[8,144,128]{2,1,0:T(8,128)(2,1)}), f16[8,144,128]{2,1,0:T(8,128)(2,1)}, u32[]{:S(2)}, u32[]{:S(2)}) async-start(f16[8,144,128]{2,1,0:T(8,128)(2,1)} %convert_element_type.38), calls=%async_computation.2 | async-start | bytes 589824 | tf_op jit(solution)/shard_map/all_to_all | solution.py:457
  45.0 2.2 %copy-start.5 = (f32[2,64,1024]{2,1,0:T(8,128)}, f32[2,64,1024]{2,1,0:T(8,128)S(1)}, u32[]{:S(2)}) copy-start(f32[2,64,1024]{2,1,0:T(8,128)S(1)} %add.13) | copy-start | bytes 1572868
  45.1 26.7 %collective-permute-start.1 = (f32[64,1024]{1,0:T(8,128)S(1)}, f32[64,1024]{1,0:T(8,128)S(1)}, u32[]{:S(2)}, u32[]{:S(2)}) collective-permute-start(f32[64,1024]{1,0:T(8,128)S(1)} %slice_bitcast_fusion), channel_id=1, source_target_pairs={{0,2},{1,3},{2,0},{3,1},{4,6},{5,7},{6,4},{7,5},{8,10},{9,11},{10,... | collective-permute-start | bytes 786440 | tf_op jit(solution)/shard_map/ppermute | solution.py:459
  56.7 8.3 %collective-permute-start.6 = (f16[528,128]{1,0:T(8,128)(2,1)S(1)}, f16[528,128]{1,0:T(8,128)(2,1)S(1)}, u32[]{:S(2)}, u32[]{:S(2)}) collective-permute-start(f16[528,128]{1,0:T(8,128)(2,1)S(1)} %convert_element_type.36), channel_id=1, source_target_pairs={{0,24},{4,28},{8,16},{12,20},{16,8},{20,12},{24,0},{28,4},{1,25},{... | collective-permute-start | bytes 405512 | tf_op jit(solution)/shard_map/ppermute | solution.py:447
  60.1 10.8 %collective-permute-start.5 = (f16[528,128]{1,0:T(8,128)(2,1)S(1)}, f16[528,128]{1,0:T(8,128)(2,1)S(1)}, u32[]{:S(2)}, u32[]{:S(2)}) collective-permute-start(f16[528,128]{1,0:T(8,128)(2,1)S(1)} %convert_element_type.34), channel_id=1, source_target_pairs={{0,16},{4,20},{8,24},{12,28},{16,0},{20,4},{24,8},{28,12},{1,17},{... | collective-permute-start | bytes 405512 | tf_op jit(solution)/shard_map/ppermute | solution.py:447
  60.1 10.8 %collective-permute-start.4 = (f16[528,128]{1,0:T(8,128)(2,1)S(1)}, f16[528,128]{1,0:T(8,128)(2,1)S(1)}, u32[]{:S(2)}, u32[]{:S(2)}) collective-permute-start(f16[528,128]{1,0:T(8,128)(2,1)S(1)} %convert_element_type.32), channel_id=1, source_target_pairs={{0,8},{4,12},{8,0},{12,4},{16,24},{20,28},{24,16},{28,20},{1,9},{5... | collective-permute-start | bytes 405512 | tf_op jit(solution)/shard_map/ppermute | solution.py:447
  71.0 1.1 %copy-start.6 = (f32[2,64,1024]{2,1,0:T(8,128)S(1)}, f32[2,64,1024]{2,1,0:T(8,128)}, u32[]{:S(2)}) copy-start(f32[2,64,1024]{2,1,0:T(8,128)} %copy-done.5) | copy-start | bytes 1572868

commit v2 on v1

--- a/solution.py
+++ b/solution.py
@@ -148,31 +148,20 @@
 
 
 def keyval_kernel(send_hbm, x_hbm, wkv_hbm, out_ref, x_ref, wkv_ref, send_ref, kv_ref, sems):
-    rows = out_ref.shape[1]
-    chunks = sems.shape[1]
-    depth = x_ref.shape[1] // chunks
+    tiles, rows = kv_ref.shape[:2]
+    weight = pltpu.make_async_copy(wkv_hbm, wkv_ref, sems.at[0])
+    listing = pltpu.make_async_copy(send_hbm, send_ref, sems.at[1])
+    weight.start()
     copies = []
-    for c in range(chunks):
-        at = pl.ds(c * depth, depth)
-        pair = (
-            pltpu.make_async_copy(x_hbm.at[:, at], x_ref.at[:, at], sems.at[0, c]),
-            pltpu.make_async_copy(wkv_hbm.at[at], wkv_ref.at[at], sems.at[1, c]),
-        )
-        for copy in pair:
-            copy.start()
-        copies.append(pair)
-    listing = pltpu.make_async_copy(send_hbm, send_ref, sems.at[2, 0])
+    for t in range(tiles):
+        at = pl.ds(t * rows, rows)
+        copies.append(pltpu.make_async_copy(x_hbm.at[at], x_ref.at[at], sems.at[2 + t]))
+        copies[-1].start()
     listing.start()
-    kv = None
-    for c, pair in enumerate(copies):
-        for copy in pair:
-            copy.wait()
-        at = pl.ds(c * depth, depth)
-        part = dot(x_ref[:, at], wkv_ref[at])
-        kv = part if kv is None else kv + part
-    kv = kv.astype(BF16)
-    for t in range(kv_ref.shape[0]):
-        kv_ref[t] = kv[t * rows : (t + 1) * rows]
+    weight.wait()
+    for t, copy in enumerate(copies):
+        copy.wait()
+        kv_ref[t] = dot(x_ref[t * rows : (t + 1) * rows], wkv_ref[...]).astype(BF16)
     listing.wait()
     for r in range(out_ref.shape[0]):
         out_ref[r] = kv_ref[send_ref[r]]
@@ -363,55 +352,51 @@
     wo2 = wo.reshape(head_width, width)
 
     outgoing = pl.pallas_call(
-        keyval_kernel,
-        out_shape=jax.ShapeDtypeStruct((parts, rows, kv_width), BF16),
-        in_specs=[pl.BlockSpec(memory_space=pltpu.HBM)] * 3,
-        out_specs=vmem(1)[0],
-        scratch_shapes=[
-            pltpu.VMEM(x.shape, BF16),
-            pltpu.VMEM(wkv2.shape, BF16),
-            pltpu.SMEM(send.shape, jnp.int32),
-            pltpu.VMEM((tiles, rows, kv_width), BF16),
-            pltpu.SemaphoreType.DMA((3, 4)),
-        ],
-        name="keyval",
+keyval_kernel,
+out_shape=jax.ShapeDtypeStruct((parts, rows, kv_width), BF16),
+in_specs=[pl.BlockSpec(memory_space=pltpu.HBM)] * 3,
+out_specs=vmem(1)[0],
+scratch_shapes=[
+    pltpu.VMEM(x.shape, BF16),
+    pltpu.VMEM(wkv2.shape, BF16),
+    pltpu.SMEM(send.shape, jnp.int32),
+    pltpu.VMEM((tiles, rows, kv_width), BF16),
+    pltpu.SemaphoreType.DMA((2 + tiles,)),
+],
     )(send, x, wkv2)
     received = lax.all_to_all(outgoing, "graph", split_axis=0, concat_axis=0, tiled=True)
     keys = parts * rows
     share = tokens // mp
     outer = parts // 2
     weights = pl.pallas_call(
-        project_kernel,
-        out_shape=jax.ShapeDtypeStruct((groups, kv_width, 2 * tokens), BF16),
-        in_specs=vmem(4),
-        out_specs=vmem(1)[0],
-        compiler_params=GRANT,
-        name="project",
+project_kernel,
+out_shape=jax.ShapeDtypeStruct((groups, kv_width, 2 * tokens), BF16),
+in_specs=vmem(4),
+out_specs=vmem(1)[0],
+compiler_params=GRANT,
     )(x, wq2, wo2, cotangent)
     half = pl.pallas_call(
-        halves_kernel,
-        out_shape=jax.ShapeDtypeStruct((2, outer, tokens, cols), BF16),
-        in_specs=vmem(2),
-        out_specs=vmem(1)[0],
-        compiler_params=GRANT,
-        name="halves",
+halves_kernel,
+out_shape=jax.ShapeDtypeStruct((2, outer, tokens, cols), BF16),
+in_specs=vmem(2),
+out_specs=vmem(1)[0],
+compiler_params=GRANT,
     )(cotangent, x)
     half_got = lax.ppermute(half, "graph", xor_pairs(parts, 1))
     slot_grad, mix = pl.pallas_call(
-        attention_kernel,
-        out_shape=(
-            jax.ShapeDtypeStruct((keys, kv_width), BF16),
-            jax.ShapeDtypeStruct((2, groups, DH, tokens), BF16),
-        ),
-        in_specs=vmem(2),
-        out_specs=tuple(vmem(2)),
-        scratch_shapes=[
-            pltpu.VMEM((keys, kv_width), F32),
-            pltpu.VMEM((2, keys, 2 * tokens), F32),
-            pltpu.VMEM((2, keys, 2 * tokens), BF16),
-        ],
-        compiler_params=WIDE,
-        name="attention",
+attention_kernel,
+out_shape=(
+jax.ShapeDtypeStruct((keys, kv_width), BF16),
+jax.ShapeDtypeStruct((2, groups, DH, tokens), BF16),
+),
+in_specs=vmem(2),
+out_specs=tuple(vmem(2)),
+scratch_shapes=[
+pltpu.VMEM((keys, kv_width), F32),
+pltpu.VMEM((2, keys, 2 * tokens), F32),
+pltpu.VMEM((2, keys, 2 * tokens), BF16),
+],
+compiler_params=WIDE,
     )(weights, received.reshape(keys, kv_width))
     returned = lax.all_to_all(
         slot_grad.reshape(parts, rows, kv_width), "graph", split_axis=0, concat_axis=0, tiled=True
@@ -419,39 +404,36 @@
     mix = mix.reshape(2, head_width, tokens)
     mix_got = lax.ppermute(mix, "graph", xor_pairs(parts, 1))
     out_keep, out_away = pl.pallas_call(
-        output_kernel,
-        out_shape=(
-            jax.ShapeDtypeStruct((mp // 2, share, width), F32),
-            jax.ShapeDtypeStruct((mp // 2, share, width), F32),
-        ),
-        in_specs=vmem(2),
-        out_specs=tuple(vmem(2)),
-        compiler_params=GRANT,
-        name="output",
+output_kernel,
+out_shape=(
+jax.ShapeDtypeStruct((mp // 2, share, width), F32),
+jax.ShapeDtypeStruct((mp // 2, share, width), F32),
+),
+in_specs=vmem(2),
+out_specs=tuple(vmem(2)),
+compiler_params=GRANT,
     )(mix, wo2)
     out_got = lax.ppermute(out_away, "mp", xor_pairs(mp, 1))
     sums, *sums_away = pl.pallas_call(
-        weights_kernel,
-        out_shape=tuple(
-            jax.ShapeDtypeStruct((2 * head_width + 16 * (d > 0), cols), F32)
-            for d in range(outer)
-        ),
-        in_specs=vmem(5),
-        out_specs=tuple(vmem(outer)),
-        compiler_params=GRANT,
-        name="weights",
+weights_kernel,
+out_shape=tuple(
+jax.ShapeDtypeStruct((2 * head_width + 16 * (d > 0), cols), F32)
+for d in range(outer)
+),
+in_specs=vmem(5),
+out_specs=tuple(vmem(outer)),
+compiler_params=GRANT,
     )(mix, mix_got, cotangent, x, half_got)
     sums_got = []
     for d in range(1, outer):
         away = sums_away[d - 1].astype(jnp.float16)
         sums_got.append(lax.ppermute(away, "graph", xor_pairs(parts, 2 * d)))
     kv_parts = pl.pallas_call(
-        owner_kernel,
-        out_shape=jax.ShapeDtypeStruct((parts, kv_width + 16, cols), F32),
-        in_specs=[SMEM] + vmem(2),
-        out_specs=vmem(1)[0],
-        compiler_params=GRANT,
-        name="owner",
+owner_kernel,
+out_shape=jax.ShapeDtypeStruct((parts, kv_width + 16, cols), F32),
+in_specs=[SMEM] + vmem(2),
+out_specs=vmem(1)[0],
+compiler_params=GRANT,
     )(send, returned, x)
     kv_parts = kv_parts.astype(jnp.float16)
     kv_got = lax.all_to_all(kv_parts, "graph", split_axis=0, concat_axis=0, tiled=True)
@@ -460,20 +442,18 @@
     own_rows = lax.dynamic_slice_in_dim(x, lax.axis_index("mp") * share, share, 0)
     output = (own_rows.astype(F32) + (out_half[0] + out_last)).astype(BF16)
     grad_wo, grad_wq = pl.pallas_call(
-        sums_kernel,
-        out_shape=tuple(jax.ShapeDtypeStruct((head_width, cols), F32) for _ in range(2)),
-        in_specs=vmem(outer),
-        out_specs=tuple(vmem(2)),
-        compiler_params=GRANT,
-        name="sums",
+sums_kernel,
+out_shape=tuple(jax.ShapeDtypeStruct((head_width, cols), F32) for _ in range(2)),
+in_specs=vmem(outer),
+out_specs=tuple(vmem(2)),
+compiler_params=GRANT,
     )(sums, *(got.astype(F32) for got in sums_got))
     grad_wkv = pl.pallas_call(
-        kvsum_kernel,
-        out_shape=jax.ShapeDtypeStruct((kv_width, cols), F32),
-        in_specs=vmem(1),
-        out_specs=vmem(1)[0],
-        compiler_params=GRANT,
-        name="kvsum",
+kvsum_kernel,
+out_shape=jax.ShapeDtypeStruct((kv_width, cols), F32),
+in_specs=vmem(1),
+out_specs=vmem(1)[0],
+compiler_params=GRANT,
     )(kv_got.astype(F32))
     return (
         output,

time: 75.2 us -> 75 us (level)
  no operation moved by 1% of the time
where the time goes in v2:
time: 75 us; the launch traced here: 74.3 us
  waiting for transfers between devices  32.6 us (43%)
  starting transfers between devices  23.3 us (31%)
  Pallas kernels  13.5 us (18%)
  other arithmetic  2.67 us (4%)
  local copies, waits for them, and re-layouts  1.44 us (2%)
  between operations  0.82 us (1%)
    ppermute x3, waiting for transfers between devices, shared_local(): sums_got.append(lax.ppermute(away, 'graph', xor_pairs(parts, 2 * d)))  9.65 us
    ppermute x1, waiting for transfers between devices, shared_local(): mix_got = lax.ppermute(mix, 'graph', xor_pairs(parts, 1))  7.54 us
    all_to_all x1, starting transfers between devices, shared_local(): lax.all_to_all(outgoing, 'graph', split_axis=0, concat_axis=0, tiled=True)  7.45 us
    all_to_all x1, waiting for transfers between devices, shared_local(): lax.all_to_all(slot_grad.reshape(parts, rows, kv_width), 'graph', split_a...  7.43 us
    all_to_all x1, waiting for transfers between devices, shared_local(): lax.all_to_all(outgoing, 'graph', split_axis=0, concat_axis=0, tiled=True)  7.36 us
    pallas_call x1, Pallas kernels, shared_local(): pl.pallas_call(attention_kernel, out_shape=(jax.ShapeDtypeStruct((keys, k...  4.94 us
    ppermute x3, starting transfers between devices, shared_local(): sums_got.append(lax.ppermute(away, 'graph', xor_pairs(parts, 2 * d)))  4.52 us
    all_to_all x1, starting transfers between devices, shared_local(): lax.all_to_all(kv_parts, 'graph', split_axis=0, concat_axis=0, tiled=True)  4.06 us
  transfers between devices with their start and end apart: 10, of which 6 were waited for; matrix products, arithmetic and copies ran while one was open for 2% of the time, Pallas kernels for 6%

profile of v2, /device:TPU:0, one launch (start us, length us, event | category | flops | bytes accessed | tf_op | source)
XLA Modules:
  0.0 74.3 jit_solution(7427910218393890785)
XLA Ops:
  0.6 0.0 copy-start.1
  0.6 0.0 copy-start.2
  0.7 2.3 %shard_map.94 = bf16[8,128,128]{2,1,0:T(8,128)(2,1)} custom-call(s32[8]{0:T(128)} %bitcast.36, bf16[256,1024]{1,0:T(8,128)(2,1)} %bitcast.23, bf16[1024,128]{1,0:T(8,128)(2,1)} %bitcast.38), custom_call_target="tpu_custom_call" | custom-call | tf_op jit(solution)/shard_map/pallas_call | solution.py:354
  3.0 0.0 copy-start
  3.0 7.5 %all-to-all-start = ((bf16[8,128,128]{2,1,0:T(8,128)(2,1)}), bf16[8,128,128]{2,1,0:T(8,128)(2,1)S(1)}, u32[]{:S(2)}, u32[]{:S(2)}) async-start(bf16[8,128,128]{2,1,0:T(8,128)(2,1)} %shard_map.94), calls=%async_computation | async-start | bytes 524288 | tf_op jit(solution)/shard_map/all_to_all | solution.py:367
  10.4 0.0 copy-done.1
  10.4 0.0 copy-done.2
  10.5 0.0 copy-done
  10.5 0.0 copy-start.3
  10.5 1.0 %copy-done.3 = bf16[1024,1,256]{2,0,1:T(8,128)(2,1)S(1)} copy-done((bf16[1024,1,256]{2,0,1:T(8,128)(2,1)S(1)}, bf16[1024,1,256]{2,0,1:T(8,128)(2,1)}, u32[]{:S(2)}) %copy-start.3) | copy-done | bytes 524312
  11.5 0.5 shard_map.93.w_ref
  12.0 7.4 %all-to-all-done = bf16[8,128,128]{2,1,0:T(8,128)(2,1)S(1)} async-done(((bf16[8,128,128]{2,1,0:T(8,128)(2,1)}), bf16[8,128,128]{2,1,0:T(8,128)(2,1)S(1)}, u32[]{:S(2)}, u32[]{:S(2)}) %all-to-all-start) | async-done | bytes 262176 | tf_op jit(solution)/shard_map/all_to_all | solution.py:367
  19.4 4.9 %shard_map.95 = (bf16[1024,128]{1,0:T(8,128)(2,1)}, bf16[2,4,64,256]{3,2,1,0:T(8,128)(2,1)S(1)}) custom-call(bf16[4,128,512]{2,1,0:T(8,128)(2,1)S(1)} %shard_map.93.w_ref, bf16[1024,128]{1,0:T(8,128)(2,1)S(1)} %bitcast.31), custom_call_target="tpu_custom_call" | custom-call | tf_op jit(solution)/shard_map/pallas_call | solution.py:386
  24.3 1.2 %shard_map.96 = (f32[2,64,1024]{2,1,0:T(8,128)S(1)}, f32[2,64,1024]{2,1,0:T(8,128)}) custom-call(bf16[2,256,256]{2,1,0:T(8,128)(2,1)S(1)} %bitcast.32, bf16[256,1024]{1,0:T(8,128)(2,1)S(1)} %bitcast.30), custom_call_target="tpu_custom_call" | custom-call | tf_op jit(solution)/shard_map/pallas_call | solution.py:406
  25.5 0.0 collective-permute-start
  25.5 3.6 %all-to-all-start.1 = ((bf16[8,128,128]{2,1,0:T(8,128)(2,1)}), bf16[8,128,128]{2,1,0:T(8,128)(2,1)S(1)}, u32[]{:S(2)}, u32[]{:S(2)}) async-start(bf16[8,128,128]{2,1,0:T(8,128)(2,1)} %bitcast.10), calls=%async_computation.1 | async-start | bytes 524288 | tf_op jit(solution)/shard_map/all_to_all | solution.py:401
  29.1 0.0 copy-start.4
  29.1 0.2 shard_map.97
  29.2 2.1 %collective-permute-start.3 = (bf16[2,4,256,128]{3,2,1,0:T(8,128)(2,1)S(1)}, bf16[2,4,256,128]{3,2,1,0:T(8,128)(2,1)}, u32[]{:S(2)}, u32[]{:S(2)}) collective-permute-start(bf16[2,4,256,128]{3,2,1,0:T(8,128)(2,1)S(1)} %shard_map.97), channel_id=1, source_target_pairs={{0,4},{4,0},{8,12},{12,8},{16,20},{20,16},{24,28},{28,24},{1,5},{5... | collective-permute-start | bytes 1572872 | tf_op jit(solution)/shard_map/ppermute | solution.py:385
  31.3 0.1 collective-permute-start.2
  31.4 7.4 %all-to-all-done.1.ret_ref = bf16[8,128,128]{2,1,0:T(8,128)(2,1)S(1)} async-done(((bf16[8,128,128]{2,1,0:T(8,128)(2,1)}), bf16[8,128,128]{2,1,0:T(8,128)(2,1)S(1)}, u32[]{:S(2)}, u32[]{:S(2)}) %all-to-all-start.1) | async-done | bytes 262176 | tf_op jit(solution)/shard_map/all_to_all | solution.py:401
  38.8 0.0 copy-done.4
  38.8 1.1 %shard_map.100 = f32[8,144,128]{2,1,0:T(8,128)S(1)} custom-call(s32[8]{0:T(128)S(1)} %bitcast.37, bf16[8,128,128]{2,1,0:T(8,128)(2,1)S(1)} %all-to-all-done.1.ret_ref, bf16[256,1024]{1,0:T(8,128)(2,1)S(1)} %bitcast.26), custom_call_target="tpu_custom_call" | custom-call | tf_op jit(solution)/shard_map/pallas_call | solution.py:431
  39.9 0.8 %convert_element_type.38 = f16[8,144,128]{2,1,0:T(8,128)(2,1)} convert(f32[8,144,128]{2,1,0:T(8,128)S(1)} %shard_map.100) | non-fusion elementwise | flops 147456 | bytes 884736 | tf_op jit(solution)/shard_map/convert_element_type | solution.py:438
  40.6 4.1 %all-to-all-start.2 = ((f16[8,144,128]{2,1,0:T(8,128)(2,1)}), f16[8,144,128]{2,1,0:T(8,128)(2,1)}, u32[]{:S(2)}, u32[]{:S(2)}) async-start(f16[8,144,128]{2,1,0:T(8,128)(2,1)} %convert_element_type.38), calls=%async_computation.2 | async-start | bytes 589824 | tf_op jit(solution)/shard_map/all_to_all | solution.py:439
  44.7 0.0 collective-permute-done
  44.7 0.1 add.13
  44.8 0.0 copy-start.5
  44.8 1.6 %collective-permute-start.1 = (f32[64,1024]{1,0:T(8,128)S(1)}, f32[64,1024]{1,0:T(8,128)S(1)}, u32[]{:S(2)}, u32[]{:S(2)}) collective-permute-start(f32[64,1024]{1,0:T(8,128)S(1)} %slice_bitcast_fusion), channel_id=1, source_target_pairs={{0,2},{1,3},{2,0},{3,1},{4,6},{5,7},{6,4},{7,5},{8,10},{9,11},{10,... | collective-permute-start | bytes 786440 | tf_op jit(solution)/shard_map/ppermute | solution.py:441
  46.4 0.6 collective-permute-done.3.half_ref
  47.0 0.0 copy-done.5
  47.0 7.5 %collective-permute-done.2.mix_got_ref = bf16[2,256,256]{2,1,0:T(8,128)(2,1)S(1)} collective-permute-done((bf16[2,256,256]{2,1,0:T(8,128)(2,1)S(1)}, bf16[2,256,256]{2,1,0:T(8,128)(2,1)S(1)}, u32[]{:S(2)}, u32[]{:S(2)}) %collective-permute-start.2) | collective-permute-done | bytes 262176 | tf_op jit(solution)/shard_map/ppermute | solution.py:405
  54.5 1.9 %shard_map.98 = (f32[512,128]{1,0:T(8,128)S(1)}, f32[528,128]{1,0:T(8,128)S(1)}, f32[528,128]{1,0:T(8,128)S(1)}, f32[528,128]{1,0:T(8,128)S(1)}) custom-call(bf16[2,256,256]{2,1,0:T(8,128)(2,1)S(1)} %bitcast.34, bf16[2,256,256]{2,1,0:T(8,128)(2,1)S(1)} %collective-permute-done.2.mix_got_ref, bf16[256,1024]{1,0:T(8,128)(2,1)S(1)} %copy-done.1, ...), custom_call_target="tpu_custom_call" | custom-call | tf_op jit(solution)/shard_map/pallas_call | solution.py:417
  56.5 3.4 %collective-permute-start.6 = (f16[528,128]{1,0:T(8,128)(2,1)S(1)}, f16[528,128]{1,0:T(8,128)(2,1)S(1)}, u32[]{:S(2)}, u32[]{:S(2)}) collective-permute-start(f16[528,128]{1,0:T(8,128)(2,1)S(1)} %convert_element_type.36), channel_id=1, source_target_pairs={{0,24},{4,28},{8,16},{12,20},{16,8},{20,12},{24,0},{28,4},{1,25},{... | collective-permute-start | bytes 405512 | tf_op jit(solution)/shard_map/ppermute | solution.py:430
  59.9 0.0 collective-permute-start.5
  59.9 1.1 %collective-permute-start.4 = (f16[528,128]{1,0:T(8,128)(2,1)S(1)}, f16[528,128]{1,0:T(8,128)(2,1)S(1)}, u32[]{:S(2)}, u32[]{:S(2)}) collective-permute-start(f16[528,128]{1,0:T(8,128)(2,1)S(1)} %convert_element_type.32), channel_id=1, source_target_pairs={{0,8},{4,12},{8,0},{12,4},{16,24},{20,28},{24,16},{28,20},{1,9},{5... | collective-permute-start | bytes 405512 | tf_op jit(solution)/shard_map/ppermute | solution.py:430
  61.1 3.8 %collective-permute-done.6 = f16[528,128]{1,0:T(8,128)(2,1)S(1)} collective-permute-done((f16[528,128]{1,0:T(8,128)(2,1)S(1)}, f16[528,128]{1,0:T(8,128)(2,1)S(1)}, u32[]{:S(2)}, u32[]{:S(2)}) %collective-permute-start.6) | collective-permute-done | bytes 135200 | tf_op jit(solution)/shard_map/ppermute | solution.py:430
  64.9 5.9 %collective-permute-done.5 = f16[528,128]{1,0:T(8,128)(2,1)S(1)} collective-permute-done((f16[528,128]{1,0:T(8,128)(2,1)S(1)}, f16[528,128]{1,0:T(8,128)(2,1)S(1)}, u32[]{:S(2)}, u32[]{:S(2)}) %collective-permute-start.5) | collective-permute-done | bytes 135200 | tf_op jit(solution)/shard_map/ppermute | solution.py:430
  70.8 0.0 collective-permute-done.4
  70.8 0.0 copy-start.6
  70.8 0.8 %shard_map.99 = (f32[256,128]{1,0:T(8,128)}, f32[256,128]{1,0:T(8,128)}) custom-call(f32[512,128]{1,0:T(8,128)S(1)} %get-tuple-element.17.own_ref, f32[528,128]{1,0:T(8,128)S(1)} %convert_element_type.33.refs_0_, f32[528,128]{1,0:T(8,128)S(1)} %convert_element_type.35.refs_1_, f32[528,128]{1,0:T(8,128)S(1)} %convert_element_type.37.refs_2_), custom_call_target="tpu_custom_call" | custom-call | tf_op jit(solution)/shard_map/pallas_call | solution.py:444
  71.6 0.0 collective-permute-done.1
  71.6 0.4 copy-done.6
  71.9 0.7 fusion.2
  72.6 0.0 all-to-all-done.2
  72.7 1.0 %convert_element_type.39.got_ref = f32[8,144,128]{2,1,0:T(8,128)S(1)} convert(f16[8,144,128]{2,1,0:T(8,128)(2,1)} %all-to-all-done.2) | non-fusion elementwise | flops 147456 | bytes 884736 | tf_op jit(solution)/shard_map/convert_element_type | solution.py:457
  73.7 0.7 shard_map.101
  (7 shorter events, 0.1 us)
Async XLA Ops:
  0.6 9.8 %copy-start.1 = (bf16[256,1024]{1,0:T(8,128)(2,1)S(1)}, bf16[256,1024]{1,0:T(8,128)(2,1)}, u32[]{:S(2)}) copy-start(bf16[256,1024]{1,0:T(8,128)(2,1)} %cot_ref.5) | copy-start | bytes 1572868
  0.6 9.8 %copy-start.2 = (bf16[1,256,1024]{2,1,0:T(8,128)(2,1)S(1)}, bf16[1,256,1024]{2,1,0:T(8,128)(2,1)}, u32[]{:S(2)}) copy-start(bf16[1,256,1024]{2,1,0:T(8,128)(2,1)} %param.10) | copy-start | bytes 1572868
  3.0 7.5 %copy-start = (bf16[2,128,1024]{2,1,0:T(8,128)(2,1)S(1)}, bf16[2,128,1024]{2,1,0:T(8,128)(2,1)}, u32[]{:S(2)}) copy-start(bf16[2,128,1024]{2,1,0:T(8,128)(2,1)} %param.7) | copy-start | bytes 1572868
  3.0 16.4 %all-to-all-start = ((bf16[8,128,128]{2,1,0:T(8,128)(2,1)}), bf16[8,128,128]{2,1,0:T(8,128)(2,1)S(1)}, u32[]{:S(2)}, u32[]{:S(2)}) async-start(bf16[8,128,128]{2,1,0:T(8,128)(2,1)} %shard_map.94), calls=%async_computation | async-start | bytes 524288 | tf_op jit(solution)/shard_map/all_to_all | solution.py:367
  10.5 1.0 %copy-start.3 = (bf16[1024,1,256]{2,0,1:T(8,128)(2,1)S(1)}, bf16[1024,1,256]{2,0,1:T(8,128)(2,1)}, u32[]{:S(2)}) copy-start(bf16[1024,1,256]{2,0,1:T(8,128)(2,1)} %param.8) | copy-start | bytes 1572868
  25.5 19.2 %collective-permute-start = (f32[2,64,1024]{2,1,0:T(8,128)}, f32[2,64,1024]{2,1,0:T(8,128)S(1)}, u32[]{:S(2)}, u32[]{:S(2)}) collective-permute-start(f32[2,64,1024]{2,1,0:T(8,128)} %get-tuple-element.16), channel_id=1, source_target_pairs={{0,1},{1,0},{2,3},{3,2},{4,5},{5,4},{6,7},{7,6},{8,9},{9,8},{10,11... | collective-permute-start | bytes 1572872 | tf_op jit(solution)/shard_map/ppermute | solution.py:416
  25.5 13.3 %all-to-all-start.1 = ((bf16[8,128,128]{2,1,0:T(8,128)(2,1)}), bf16[8,128,128]{2,1,0:T(8,128)(2,1)S(1)}, u32[]{:S(2)}, u32[]{:S(2)}) async-start(bf16[8,128,128]{2,1,0:T(8,128)(2,1)} %bitcast.10), calls=%async_computation.1 | async-start | bytes 524288 | tf_op jit(solution)/shard_map/all_to_all | solution.py:401
  29.1 9.7 %copy-start.4 = (s32[1,8,1]{1,2,0:T(1,128)S(1)}, s32[1,8,1]{1,2,0:T(1,128)}, u32[]{:S(2)}) copy-start(s32[1,8,1]{1,2,0:T(1,128)} %param.11) | copy-start | bytes 100
  29.2 17.7 %collective-permute-start.3 = (bf16[2,4,256,128]{3,2,1,0:T(8,128)(2,1)S(1)}, bf16[2,4,256,128]{3,2,1,0:T(8,128)(2,1)}, u32[]{:S(2)}, u32[]{:S(2)}) collective-permute-start(bf16[2,4,256,128]{3,2,1,0:T(8,128)(2,1)S(1)} %shard_map.97), channel_id=1, source_target_pairs={{0,4},{4,0},{8,12},{12,8},{16,20},{20,16},{24,28},{28,24},{1,5},{5... | collective-permute-start | bytes 1572872 | tf_op jit(solution)/shard_map/ppermute | solution.py:385
  31.3 23.2 %collective-permute-start.2 = (bf16[2,256,256]{2,1,0:T(8,128)(2,1)S(1)}, bf16[2,256,256]{2,1,0:T(8,128)(2,1)S(1)}, u32[]{:S(2)}, u32[]{:S(2)}) collective-permute-start(bf16[2,256,256]{2,1,0:T(8,128)(2,1)S(1)} %bitcast.33), channel_id=1, source_target_pairs={{0,4},{4,0},{8,12},{12,8},{16,20},{20,16},{24,28},{28,24},{1,5},{5... | collective-permute-start | bytes 786440 | tf_op jit(solution)/shard_map/ppermute | solution.py:405
  40.6 32.0 %all-to-all-start.2 = ((f16[8,144,128]{2,1,0:T(8,128)(2,1)}), f16[8,144,128]{2,1,0:T(8,128)(2,1)}, u32[]{:S(2)}, u32[]{:S(2)}) async-start(f16[8,144,128]{2,1,0:T(8,128)(2,1)} %convert_element_type.38), calls=%async_computation.2 | async-start | bytes 589824 | tf_op jit(solution)/shard_map/all_to_all | solution.py:439
  44.8 2.2 %copy-start.5 = (f32[2,64,1024]{2,1,0:T(8,128)}, f32[2,64,1024]{2,1,0:T(8,128)S(1)}, u32[]{:S(2)}) copy-start(f32[2,64,1024]{2,1,0:T(8,128)S(1)} %add.13) | copy-start | bytes 1572868
  44.8 26.7 %collective-permute-start.1 = (f32[64,1024]{1,0:T(8,128)S(1)}, f32[64,1024]{1,0:T(8,128)S(1)}, u32[]{:S(2)}, u32[]{:S(2)}) collective-permute-start(f32[64,1024]{1,0:T(8,128)S(1)} %slice_bitcast_fusion), channel_id=1, source_target_pairs={{0,2},{1,3},{2,0},{3,1},{4,6},{5,7},{6,4},{7,5},{8,10},{9,11},{10,... | collective-permute-start | bytes 786440 | tf_op jit(solution)/shard_map/ppermute | solution.py:441
  56.5 8.3 %collective-permute-start.6 = (f16[528,128]{1,0:T(8,128)(2,1)S(1)}, f16[528,128]{1,0:T(8,128)(2,1)S(1)}, u32[]{:S(2)}, u32[]{:S(2)}) collective-permute-start(f16[528,128]{1,0:T(8,128)(2,1)S(1)} %convert_element_type.36), channel_id=1, source_target_pairs={{0,24},{4,28},{8,16},{12,20},{16,8},{20,12},{24,0},{28,4},{1,25},{... | collective-permute-start | bytes 405512 | tf_op jit(solution)/shard_map/ppermute | solution.py:430
  59.9 10.8 %collective-permute-start.5 = (f16[528,128]{1,0:T(8,128)(2,1)S(1)}, f16[528,128]{1,0:T(8,128)(2,1)S(1)}, u32[]{:S(2)}, u32[]{:S(2)}) collective-permute-start(f16[528,128]{1,0:T(8,128)(2,1)S(1)} %convert_element_type.34), channel_id=1, source_target_pairs={{0,16},{4,20},{8,24},{12,28},{16,0},{20,4},{24,8},{28,12},{1,17},{... | collective-permute-start | bytes 405512 | tf_op jit(solution)/shard_map/ppermute | solution.py:430
  59.9 10.8 %collective-permute-start.4 = (f16[528,128]{1,0:T(8,128)(2,1)S(1)}, f16[528,128]{1,0:T(8,128)(2,1)S(1)}, u32[]{:S(2)}, u32[]{:S(2)}) collective-permute-start(f16[528,128]{1,0:T(8,128)(2,1)S(1)} %convert_element_type.32), channel_id=1, source_target_pairs={{0,8},{4,12},{8,0},{12,4},{16,24},{20,28},{24,16},{28,20},{1,9},{5... | collective-permute-start | bytes 405512 | tf_op jit(solution)/shard_map/ppermute | solution.py:430
  70.8 1.1 %copy-start.6 = (f32[2,64,1024]{2,1,0:T(8,128)S(1)}, f32[2,64,1024]{2,1,0:T(8,128)}, u32[]{:S(2)}) copy-start(f32[2,64,1024]{2,1,0:T(8,128)} %copy-done.5) | copy-start | bytes 1572868

commit v3 on v2

--- a/solution.py
+++ b/solution.py
@@ -257,23 +257,22 @@
     y, z = lax.rem(graph, 2), lax.div(graph, 2)
     head_width = mix_ref.shape[1]
     cols = half_ref.shape[3]
-    parts = head_width // cols
     refs = (own_ref,) + out_refs
+    rows = 2 * head_width
     peak = jnp.zeros((1, 1), F32)
-    for d, ref in enumerate(refs):
-        there = lax.bitwise_xor(z, d)
-        at = pl.ds(pl.multiple_of((2 * there + y) * cols, cols), cols)
-        wo = dot(mix_ref[0], cot_ref[:, at]) + dot(mix_got_ref[0], half_ref[0, there])
-        wq = dot(mix_ref[1], x_ref[:, at]) + dot(mix_got_ref[1], half_ref[1, there])
-        ref[:head_width] = wo
-        for h in range(parts):
-            place = pl.ds(head_width + h, cols, parts)
-            ref[place, :] = wq[h * cols : (h + 1) * cols].T
-        if d > 0:
-            peak = peak_of(wo, peak_of(wq, peak))
+    for d in range(0, len(refs), 2):
+        there = [lax.bitwise_xor(z, d + i) for i in range(2)]
+        at = [pl.ds(pl.multiple_of((2 * t + y) * cols, cols), cols) for t in there]
+        for m, ref in ((0, cot_ref), (1, x_ref)):
+            mine = jnp.concatenate([ref[:, a] for a in at], axis=1)
+            theirs = jnp.concatenate([half_ref[m, t] for t in there], axis=1)
+            both = dot(mix_ref[m], mine) + dot(mix_got_ref[m], theirs)
+            for i in range(2):
+                place = slice(m * head_width, (m + 1) * head_width)
+                refs[d + i][place] = both[:, i * cols : (i + 1) * cols]
+            peak = peak_of(both, peak)
     e = exponent_of(peak)
     factor = jnp.exp2(-e)
-    rows = 2 * head_width
     for ref in out_refs:
         ref[:rows] = ref[:rows] * factor
         ref[rows:] = jnp.broadcast_to(e, ref[rows:].shape)
@@ -312,7 +311,11 @@
         total = total + unscaled(ref[...])
     half = wo_ref.shape[0]
     wo_ref[...] = total[:half]
-    wq_ref[...] = total[half:]
+    rows = wo_ref.shape[1]
+    parts = half // rows
+    for h in range(parts):
+        start = half + h * rows
+        wq_ref[pl.ds(h, rows, parts), :] = total[start : start + rows].T
 
 
 def kvsum_kernel(got_ref, out_ref):

time: 75 us -> 74.7 us (level)
  no operation moved by 1% of the time
where the time goes in v3:
time: 74.7 us; the launch traced here: 74 us
  waiting for transfers between devices  32.6 us (44%)
  starting transfers between devices  23.3 us (31%)
  Pallas kernels  13.2 us (18%)
  other arithmetic  2.67 us (4%)
  local copies, waits for them, and re-layouts  1.41 us (2%)
  between operations  0.82 us (1%)
    ppermute x3, waiting for transfers between devices, shared_local(): sums_got.append(lax.ppermute(away, 'graph', xor_pairs(parts, 2 * d)))  9.64 us
    ppermute x1, waiting for transfers between devices, shared_local(): mix_got = lax.ppermute(mix, 'graph', xor_pairs(parts, 1))  7.54 us
    all_to_all x1, starting transfers between devices, shared_local(): lax.all_to_all(outgoing, 'graph', split_axis=0, concat_axis=0, tiled=True)  7.45 us
    all_to_all x1, waiting for transfers between devices, shared_local(): lax.all_to_all(slot_grad.reshape(parts, rows, kv_width), 'graph', split_a...  7.43 us
    all_to_all x1, waiting for transfers between devices, shared_local(): lax.all_to_all(outgoing, 'graph', split_axis=0, concat_axis=0, tiled=True)  7.36 us
    pallas_call x1, Pallas kernels, shared_local(): pl.pallas_call(attention_kernel, out_shape=(jax.ShapeDtypeStruct((keys, k...  4.94 us
    ppermute x3, starting transfers between devices, shared_local(): sums_got.append(lax.ppermute(away, 'graph', xor_pairs(parts, 2 * d)))  4.52 us
    all_to_all x1, starting transfers between devices, shared_local(): lax.all_to_all(kv_parts, 'graph', split_axis=0, concat_axis=0, tiled=True)  4.06 us
  transfers between devices with their start and end apart: 10, of which 6 were waited for; matrix products, arithmetic and copies ran while one was open for 2% of the time, Pallas kernels for 6%

profile of v3, /device:TPU:0, one launch (start us, length us, event | category | flops | bytes accessed | tf_op | source)
XLA Modules:
  0.0 74.0 jit_solution(17286020620737021521)
XLA Ops:
  0.6 0.0 copy-start.1
  0.6 0.0 copy-start.2
  0.7 2.3 %shard_map.94 = bf16[8,128,128]{2,1,0:T(8,128)(2,1)} custom-call(s32[8]{0:T(128)} %bitcast.36, bf16[256,1024]{1,0:T(8,128)(2,1)} %bitcast.23, bf16[1024,128]{1,0:T(8,128)(2,1)} %bitcast.38), custom_call_target="tpu_custom_call" | custom-call | tf_op jit(solution)/shard_map/pallas_call | solution.py:357
  3.0 0.0 copy-start
  3.0 7.5 %all-to-all-start = ((bf16[8,128,128]{2,1,0:T(8,128)(2,1)}), bf16[8,128,128]{2,1,0:T(8,128)(2,1)S(1)}, u32[]{:S(2)}, u32[]{:S(2)}) async-start(bf16[8,128,128]{2,1,0:T(8,128)(2,1)} %shard_map.94), calls=%async_computation | async-start | bytes 524288 | tf_op jit(solution)/shard_map/all_to_all | solution.py:370
  10.4 0.0 copy-done.1
  10.4 0.0 copy-done.2
  10.5 0.0 copy-done
  10.5 0.0 copy-start.3
  10.5 1.0 %copy-done.3 = bf16[1024,1,256]{2,0,1:T(8,128)(2,1)S(1)} copy-done((bf16[1024,1,256]{2,0,1:T(8,128)(2,1)S(1)}, bf16[1024,1,256]{2,0,1:T(8,128)(2,1)}, u32[]{:S(2)}) %copy-start.3) | copy-done | bytes 524312
  11.5 0.5 shard_map.93.w_ref
  12.0 7.4 %all-to-all-done = bf16[8,128,128]{2,1,0:T(8,128)(2,1)S(1)} async-done(((bf16[8,128,128]{2,1,0:T(8,128)(2,1)}), bf16[8,128,128]{2,1,0:T(8,128)(2,1)S(1)}, u32[]{:S(2)}, u32[]{:S(2)}) %all-to-all-start) | async-done | bytes 262176 | tf_op jit(solution)/shard_map/all_to_all | solution.py:370
  19.4 4.9 %shard_map.95 = (bf16[1024,128]{1,0:T(8,128)(2,1)}, bf16[2,4,64,256]{3,2,1,0:T(8,128)(2,1)S(1)}) custom-call(bf16[4,128,512]{2,1,0:T(8,128)(2,1)S(1)} %shard_map.93.w_ref, bf16[1024,128]{1,0:T(8,128)(2,1)S(1)} %bitcast.31), custom_call_target="tpu_custom_call" | custom-call | tf_op jit(solution)/shard_map/pallas_call | solution.py:389
  24.3 1.2 %shard_map.96 = (f32[2,64,1024]{2,1,0:T(8,128)S(1)}, f32[2,64,1024]{2,1,0:T(8,128)}) custom-call(bf16[2,256,256]{2,1,0:T(8,128)(2,1)S(1)} %bitcast.32, bf16[256,1024]{1,0:T(8,128)(2,1)S(1)} %bitcast.30), custom_call_target="tpu_custom_call" | custom-call | tf_op jit(solution)/shard_map/pallas_call | solution.py:409
  25.5 0.0 collective-permute-start
  25.5 3.6 %all-to-all-start.1 = ((bf16[8,128,128]{2,1,0:T(8,128)(2,1)}), bf16[8,128,128]{2,1,0:T(8,128)(2,1)S(1)}, u32[]{:S(2)}, u32[]{:S(2)}) async-start(bf16[8,128,128]{2,1,0:T(8,128)(2,1)} %bitcast.10), calls=%async_computation.1 | async-start | bytes 524288 | tf_op jit(solution)/shard_map/all_to_all | solution.py:404
  29.1 0.0 copy-start.4
  29.1 0.2 shard_map.97
  29.2 2.1 %collective-permute-start.3 = (bf16[2,4,256,128]{3,2,1,0:T(8,128)(2,1)S(1)}, bf16[2,4,256,128]{3,2,1,0:T(8,128)(2,1)}, u32[]{:S(2)}, u32[]{:S(2)}) collective-permute-start(bf16[2,4,256,128]{3,2,1,0:T(8,128)(2,1)S(1)} %shard_map.97), channel_id=1, source_target_pairs={{0,4},{4,0},{8,12},{12,8},{16,20},{20,16},{24,28},{28,24},{1,5},{5... | collective-permute-start | bytes 1572872 | tf_op jit(solution)/shard_map/ppermute | solution.py:388
  31.3 0.1 collective-permute-start.2
  31.4 7.4 %all-to-all-done.1.ret_ref = bf16[8,128,128]{2,1,0:T(8,128)(2,1)S(1)} async-done(((bf16[8,128,128]{2,1,0:T(8,128)(2,1)}), bf16[8,128,128]{2,1,0:T(8,128)(2,1)S(1)}, u32[]{:S(2)}, u32[]{:S(2)}) %all-to-all-start.1) | async-done | bytes 262176 | tf_op jit(solution)/shard_map/all_to_all | solution.py:404
  38.8 0.0 copy-done.4
  38.8 1.1 %shard_map.100 = f32[8,144,128]{2,1,0:T(8,128)S(1)} custom-call(s32[8]{0:T(128)S(1)} %bitcast.37, bf16[8,128,128]{2,1,0:T(8,128)(2,1)S(1)} %all-to-all-done.1.ret_ref, bf16[256,1024]{1,0:T(8,128)(2,1)S(1)} %bitcast.26), custom_call_target="tpu_custom_call" | custom-call | tf_op jit(solution)/shard_map/pallas_call | solution.py:434
  39.9 0.8 %convert_element_type.38 = f16[8,144,128]{2,1,0:T(8,128)(2,1)} convert(f32[8,144,128]{2,1,0:T(8,128)S(1)} %shard_map.100) | non-fusion elementwise | flops 147456 | bytes 884736 | tf_op jit(solution)/shard_map/convert_element_type | solution.py:441
  40.6 4.1 %all-to-all-start.2 = ((f16[8,144,128]{2,1,0:T(8,128)(2,1)}), f16[8,144,128]{2,1,0:T(8,128)(2,1)}, u32[]{:S(2)}, u32[]{:S(2)}) async-start(f16[8,144,128]{2,1,0:T(8,128)(2,1)} %convert_element_type.38), calls=%async_computation.2 | async-start | bytes 589824 | tf_op jit(solution)/shard_map/all_to_all | solution.py:442
  44.7 0.0 collective-permute-done
  44.7 0.1 add.13
  44.8 0.0 copy-start.5
  44.8 1.6 %collective-permute-start.1 = (f32[64,1024]{1,0:T(8,128)S(1)}, f32[64,1024]{1,0:T(8,128)S(1)}, u32[]{:S(2)}, u32[]{:S(2)}) collective-permute-start(f32[64,1024]{1,0:T(8,128)S(1)} %slice_bitcast_fusion), channel_id=1, source_target_pairs={{0,2},{1,3},{2,0},{3,1},{4,6},{5,7},{6,4},{7,5},{8,10},{9,11},{10,... | collective-permute-start | bytes 786440 | tf_op jit(solution)/shard_map/ppermute | solution.py:444
  46.4 0.6 collective-permute-done.3.half_ref
  47.0 0.0 copy-done.5
  47.0 7.5 %collective-permute-done.2.mix_got_ref = bf16[2,256,256]{2,1,0:T(8,128)(2,1)S(1)} collective-permute-done((bf16[2,256,256]{2,1,0:T(8,128)(2,1)S(1)}, bf16[2,256,256]{2,1,0:T(8,128)(2,1)S(1)}, u32[]{:S(2)}, u32[]{:S(2)}) %collective-permute-start.2) | collective-permute-done | bytes 262176 | tf_op jit(solution)/shard_map/ppermute | solution.py:408
  54.5 1.6 %shard_map.98 = (f32[512,128]{1,0:T(8,128)S(1)}, f32[528,128]{1,0:T(8,128)S(1)}, f32[528,128]{1,0:T(8,128)S(1)}, f32[528,128]{1,0:T(8,128)S(1)}) custom-call(bf16[2,256,256]{2,1,0:T(8,128)(2,1)S(1)} %bitcast.34, bf16[2,256,256]{2,1,0:T(8,128)(2,1)S(1)} %collective-permute-done.2.mix_got_ref, bf16[256,1024]{1,0:T(8,128)(2,1)S(1)} %copy-done.1, ...), custom_call_target="tpu_custom_call" | custom-call | tf_op jit(solution)/shard_map/pallas_call | solution.py:420
  56.3 3.4 %collective-permute-start.6 = (f16[528,128]{1,0:T(8,128)(2,1)S(1)}, f16[528,128]{1,0:T(8,128)(2,1)S(1)}, u32[]{:S(2)}, u32[]{:S(2)}) collective-permute-start(f16[528,128]{1,0:T(8,128)(2,1)S(1)} %convert_element_type.36), channel_id=1, source_target_pairs={{0,24},{4,28},{8,16},{12,20},{16,8},{20,12},{24,0},{28,4},{1,25},{... | collective-permute-start | bytes 405512 | tf_op jit(solution)/shard_map/ppermute | solution.py:433
  59.6 0.0 collective-permute-start.5
  59.6 1.2 %collective-permute-start.4 = (f16[528,128]{1,0:T(8,128)(2,1)S(1)}, f16[528,128]{1,0:T(8,128)(2,1)S(1)}, u32[]{:S(2)}, u32[]{:S(2)}) collective-permute-start(f16[528,128]{1,0:T(8,128)(2,1)S(1)} %convert_element_type.32), channel_id=1, source_target_pairs={{0,8},{4,12},{8,0},{12,4},{16,24},{20,28},{24,16},{28,20},{1,9},{5... | collective-permute-start | bytes 405512 | tf_op jit(solution)/shard_map/ppermute | solution.py:433
  60.8 3.8 %collective-permute-done.6 = f16[528,128]{1,0:T(8,128)(2,1)S(1)} collective-permute-done((f16[528,128]{1,0:T(8,128)(2,1)S(1)}, f16[528,128]{1,0:T(8,128)(2,1)S(1)}, u32[]{:S(2)}, u32[]{:S(2)}) %collective-permute-start.6) | collective-permute-done | bytes 135200 | tf_op jit(solution)/shard_map/ppermute | solution.py:433
  64.6 5.8 %collective-permute-done.5 = f16[528,128]{1,0:T(8,128)(2,1)S(1)} collective-permute-done((f16[528,128]{1,0:T(8,128)(2,1)S(1)}, f16[528,128]{1,0:T(8,128)(2,1)S(1)}, u32[]{:S(2)}, u32[]{:S(2)}) %collective-permute-start.5) | collective-permute-done | bytes 135200 | tf_op jit(solution)/shard_map/ppermute | solution.py:433
  70.5 0.0 collective-permute-done.4
  70.5 0.0 copy-start.6
  70.5 0.8 %shard_map.99 = (f32[256,128]{1,0:T(8,128)}, f32[256,128]{1,0:T(8,128)}) custom-call(f32[512,128]{1,0:T(8,128)S(1)} %get-tuple-element.17.own_ref, f32[528,128]{1,0:T(8,128)S(1)} %convert_element_type.33.refs_0_, f32[528,128]{1,0:T(8,128)S(1)} %convert_element_type.35.refs_1_, f32[528,128]{1,0:T(8,128)S(1)} %convert_element_type.37.refs_2_), custom_call_target="tpu_custom_call" | custom-call | tf_op jit(solution)/shard_map/pallas_call | solution.py:447
  71.3 0.0 collective-permute-done.1
  71.3 0.3 copy-done.6
  71.7 0.7 fusion.2
  72.4 0.0 all-to-all-done.2
  72.4 1.0 %convert_element_type.39.got_ref = f32[8,144,128]{2,1,0:T(8,128)S(1)} convert(f16[8,144,128]{2,1,0:T(8,128)(2,1)} %all-to-all-done.2) | non-fusion elementwise | flops 147456 | bytes 884736 | tf_op jit(solution)/shard_map/convert_element_type | solution.py:460
  73.4 0.7 shard_map.101
  (7 shorter events, 0.1 us)
Async XLA Ops:
  0.6 9.8 %copy-start.1 = (bf16[256,1024]{1,0:T(8,128)(2,1)S(1)}, bf16[256,1024]{1,0:T(8,128)(2,1)}, u32[]{:S(2)}) copy-start(bf16[256,1024]{1,0:T(8,128)(2,1)} %cot_ref.5) | copy-start | bytes 1572868
  0.6 9.8 %copy-start.2 = (bf16[1,256,1024]{2,1,0:T(8,128)(2,1)S(1)}, bf16[1,256,1024]{2,1,0:T(8,128)(2,1)}, u32[]{:S(2)}) copy-start(bf16[1,256,1024]{2,1,0:T(8,128)(2,1)} %param.10) | copy-start | bytes 1572868
  3.0 7.5 %copy-start = (bf16[2,128,1024]{2,1,0:T(8,128)(2,1)S(1)}, bf16[2,128,1024]{2,1,0:T(8,128)(2,1)}, u32[]{:S(2)}) copy-start(bf16[2,128,1024]{2,1,0:T(8,128)(2,1)} %param.7) | copy-start | bytes 1572868
  3.0 16.4 %all-to-all-start = ((bf16[8,128,128]{2,1,0:T(8,128)(2,1)}), bf16[8,128,128]{2,1,0:T(8,128)(2,1)S(1)}, u32[]{:S(2)}, u32[]{:S(2)}) async-start(bf16[8,128,128]{2,1,0:T(8,128)(2,1)} %shard_map.94), calls=%async_computation | async-start | bytes 524288 | tf_op jit(solution)/shard_map/all_to_all | solution.py:370
  10.5 1.0 %copy-start.3 = (bf16[1024,1,256]{2,0,1:T(8,128)(2,1)S(1)}, bf16[1024,1,256]{2,0,1:T(8,128)(2,1)}, u32[]{:S(2)}) copy-start(bf16[1024,1,256]{2,0,1:T(8,128)(2,1)} %param.8) | copy-start | bytes 1572868
  25.5 19.2 %collective-permute-start = (f32[2,64,1024]{2,1,0:T(8,128)}, f32[2,64,1024]{2,1,0:T(8,128)S(1)}, u32[]{:S(2)}, u32[]{:S(2)}) collective-permute-start(f32[2,64,1024]{2,1,0:T(8,128)} %get-tuple-element.16), channel_id=1, source_target_pairs={{0,1},{1,0},{2,3},{3,2},{4,5},{5,4},{6,7},{7,6},{8,9},{9,8},{10,11... | collective-permute-start | bytes 1572872 | tf_op jit(solution)/shard_map/ppermute | solution.py:419
  25.5 13.3 %all-to-all-start.1 = ((bf16[8,128,128]{2,1,0:T(8,128)(2,1)}), bf16[8,128,128]{2,1,0:T(8,128)(2,1)S(1)}, u32[]{:S(2)}, u32[]{:S(2)}) async-start(bf16[8,128,128]{2,1,0:T(8,128)(2,1)} %bitcast.10), calls=%async_computation.1 | async-start | bytes 524288 | tf_op jit(solution)/shard_map/all_to_all | solution.py:404
  29.1 9.7 %copy-start.4 = (s32[1,8,1]{1,2,0:T(1,128)S(1)}, s32[1,8,1]{1,2,0:T(1,128)}, u32[]{:S(2)}) copy-start(s32[1,8,1]{1,2,0:T(1,128)} %param.11) | copy-start | bytes 100
  29.2 17.7 %collective-permute-start.3 = (bf16[2,4,256,128]{3,2,1,0:T(8,128)(2,1)S(1)}, bf16[2,4,256,128]{3,2,1,0:T(8,128)(2,1)}, u32[]{:S(2)}, u32[]{:S(2)}) collective-permute-start(bf16[2,4,256,128]{3,2,1,0:T(8,128)(2,1)S(1)} %shard_map.97), channel_id=1, source_target_pairs={{0,4},{4,0},{8,12},{12,8},{16,20},{20,16},{24,28},{28,24},{1,5},{5... | collective-permute-start | bytes 1572872 | tf_op jit(solution)/shard_map/ppermute | solution.py:388
  31.3 23.2 %collective-permute-start.2 = (bf16[2,256,256]{2,1,0:T(8,128)(2,1)S(1)}, bf16[2,256,256]{2,1,0:T(8,128)(2,1)S(1)}, u32[]{:S(2)}, u32[]{:S(2)}) collective-permute-start(bf16[2,256,256]{2,1,0:T(8,128)(2,1)S(1)} %bitcast.33), channel_id=1, source_target_pairs={{0,4},{4,0},{8,12},{12,8},{16,20},{20,16},{24,28},{28,24},{1,5},{5... | collective-permute-start | bytes 786440 | tf_op jit(solution)/shard_map/ppermute | solution.py:408
  40.6 31.7 %all-to-all-start.2 = ((f16[8,144,128]{2,1,0:T(8,128)(2,1)}), f16[8,144,128]{2,1,0:T(8,128)(2,1)}, u32[]{:S(2)}, u32[]{:S(2)}) async-start(f16[8,144,128]{2,1,0:T(8,128)(2,1)} %convert_element_type.38), calls=%async_computation.2 | async-start | bytes 589824 | tf_op jit(solution)/shard_map/all_to_all | solution.py:442
  44.8 2.2 %copy-start.5 = (f32[2,64,1024]{2,1,0:T(8,128)}, f32[2,64,1024]{2,1,0:T(8,128)S(1)}, u32[]{:S(2)}) copy-start(f32[2,64,1024]{2,1,0:T(8,128)S(1)} %add.13) | copy-start | bytes 1572868
  44.8 26.5 %collective-permute-start.1 = (f32[64,1024]{1,0:T(8,128)S(1)}, f32[64,1024]{1,0:T(8,128)S(1)}, u32[]{:S(2)}, u32[]{:S(2)}) collective-permute-start(f32[64,1024]{1,0:T(8,128)S(1)} %slice_bitcast_fusion), channel_id=1, source_target_pairs={{0,2},{1,3},{2,0},{3,1},{4,6},{5,7},{6,4},{7,5},{8,10},{9,11},{10,... | collective-permute-start | bytes 786440 | tf_op jit(solution)/shard_map/ppermute | solution.py:444
  56.3 8.3 %collective-permute-start.6 = (f16[528,128]{1,0:T(8,128)(2,1)S(1)}, f16[528,128]{1,0:T(8,128)(2,1)S(1)}, u32[]{:S(2)}, u32[]{:S(2)}) collective-permute-start(f16[528,128]{1,0:T(8,128)(2,1)S(1)} %convert_element_type.36), channel_id=1, source_target_pairs={{0,24},{4,28},{8,16},{12,20},{16,8},{20,12},{24,0},{28,4},{1,25},{... | collective-permute-start | bytes 405512 | tf_op jit(solution)/shard_map/ppermute | solution.py:433
  59.6 10.8 %collective-permute-start.5 = (f16[528,128]{1,0:T(8,128)(2,1)S(1)}, f16[528,128]{1,0:T(8,128)(2,1)S(1)}, u32[]{:S(2)}, u32[]{:S(2)}) collective-permute-start(f16[528,128]{1,0:T(8,128)(2,1)S(1)} %convert_element_type.34), channel_id=1, source_target_pairs={{0,16},{4,20},{8,24},{12,28},{16,0},{20,4},{24,8},{28,12},{1,17},{... | collective-permute-start | bytes 405512 | tf_op jit(solution)/shard_map/ppermute | solution.py:433
  59.6 10.8 %collective-permute-start.4 = (f16[528,128]{1,0:T(8,128)(2,1)S(1)}, f16[528,128]{1,0:T(8,128)(2,1)S(1)}, u32[]{:S(2)}, u32[]{:S(2)}) collective-permute-start(f16[528,128]{1,0:T(8,128)(2,1)S(1)} %convert_element_type.32), channel_id=1, source_target_pairs={{0,8},{4,12},{8,0},{12,4},{16,24},{20,28},{24,16},{28,20},{1,9},{5... | collective-permute-start | bytes 405512 | tf_op jit(solution)/shard_map/ppermute | solution.py:433
  70.5 1.1 %copy-start.6 = (f32[2,64,1024]{2,1,0:T(8,128)S(1)}, f32[2,64,1024]{2,1,0:T(8,128)}, u32[]{:S(2)}) copy-start(f32[2,64,1024]{2,1,0:T(8,128)} %copy-done.5) | copy-start | bytes 1572868
